TPU v7x, 256 devices: a whole 4x4x8 slice. The times are simulated.
256 devices in a mesh: gx: 32 (over x, z), gy: 8 (over y, core).
Axes of the slice: x: 4, y: 4, z: 8, core: 2. Of those that a mesh axis runs over, the one named last changes fastest.
Arguments:
- point_counts: int32 [512, 128, 128], P('gx', 'gy'), may hold values from 0 to 16
- face_counts: int32 [3, 512, 128, 128], P(None, 'gx', 'gy'), may hold values from -12 to 12, as said below
Outputs:
- solution: float32 [512, 128, 128], P('gx', 'gy')
- residual: float32 [512, 128, 128], P('gx', 'gy')
Inputs may be any that keep to these rules, and one draw needn't show every extreme that they name: `face_counts`: signed count of oriented points splatted onto each upper face.
All inputs are finite; a program needn't handle non-finite values.
Results may differ from a plain program's by a relative error of at most 0.0003.
Values may be sent and summed in bfloat16 or wider, within the bound.
A program may use at most 64 MiB of HBM per device.

v0:
```python
import jax
import jax.numpy as jnp
from jax import lax
from jax.sharding import PartitionSpec as P

LEVELS = 3
CYCLES = 2
COARSE_ITERS = 6


screen_weight = 0.25
flux_scale = 0.125
low_edge = 0.3
high_edge = 2.0


def padded_2(block, sides, width):
    for axis, dim in sides:
        count = lax.axis_size(axis)
        forward = [(i, i + 1) for i in range(count - 1)]
        backward = [(target, source) for source, target in forward]
        low = lax.ppermute(
            lax.slice_in_dim(block, block.shape[dim] - width, None, axis=dim), axis, forward
        )
        high = lax.ppermute(lax.slice_in_dim(block, 0, width, axis=dim), axis, backward)
        block = jnp.concatenate([low, block, high], axis=dim)
    return block


def shifted(value, axis, steps):
    count = lax.axis_size(axis)
    first, last = (max(0, -steps), min(count, count - steps))
    return lax.ppermute(value, axis, [(source, source + steps) for source in range(first, last)])


def neighbour_sum(padded):
    total = padded[2:, 1:-1, 1:-1] + padded[:-2, 1:-1, 1:-1]
    total = total + padded[1:-1, 2:, 1:-1] + padded[1:-1, :-2, 1:-1]
    total = total + padded[1:-1, 1:-1, 2:] + padded[1:-1, 1:-1, :-2]
    return total


def extend(field, level_index):
    if level_index == 0:
        padded = padded_2(field, (("gx", 0), ("gy", 1)), 1)
    elif level_index < LEVELS:
        padded = padded_2(field, (("gx", 0), ("gy", 1)), 1)
    else:
        padded = padded_2(field, (("gx", 0), ("gy", 1)), 1)
    return jnp.pad(padded, ((0, 0), (0, 0), (1, 1)))


def operate(field, screen, factor, level_index):
    return (6.0 * field - neighbour_sum(extend(field, level_index))) * factor + screen * field


def restrict(field):
    size_x, size_y, size_z = field.shape
    blocks = field.reshape(size_x // 2, 2, size_y // 2, 2, size_z // 2, 2)
    return blocks.sum(axis=(1, 3, 5)) * 0.125


def prolong(field):
    size_x, size_y, size_z = field.shape
    spread_out = jnp.broadcast_to(
        field[:, None, :, None, :, None], (size_x, 2, size_y, 2, size_z, 2)
    )
    return spread_out.reshape(2 * size_x, 2 * size_y, 2 * size_z)


def smooth(iterate, target, screen, inv_diag, factor, level_index):
    centre = 0.5 * (high_edge + low_edge)
    radius = 0.5 * (high_edge - low_edge)
    spread_ratio = centre / radius
    momentum = 1.0 / spread_ratio
    correction = (target - operate(iterate, screen, factor, level_index)) * inv_diag
    update = correction * (1.0 / centre)
    iterate = iterate + update
    momentum_next = 1.0 / (2.0 * spread_ratio - momentum)
    correction = (target - operate(iterate, screen, factor, level_index)) * inv_diag
    update = momentum_next * momentum * update + 2.0 * momentum_next / radius * correction
    iterate = iterate + update
    return iterate


def squares_total(field):
    return lax.psum(jnp.sum(field * field), ("gx", "gy"))


def spread_solve(target, screen, factor):
    iterate = jnp.zeros_like(target)
    remain = target
    search = target
    norm_now = squares_total(remain)
    for step in range(COARSE_ITERS):
        image = operate(search, screen, factor, LEVELS)
        step_length = norm_now / lax.psum(jnp.sum(search * image), ("gx", "gy"))
        iterate = iterate + step_length * search
        if step + 1 < COARSE_ITERS:
            remain = remain - step_length * image
            norm_next = squares_total(remain)
            search = remain + norm_next / norm_now * search
            norm_now = norm_next
    return iterate


def per_device(point_counts, face_counts):
    fluxes = face_counts.astype(jnp.float32) * flux_scale
    edge_x = shifted(fluxes[0, -1:].astype(jnp.bfloat16), "gx", 1).astype(jnp.float32)
    edge_y = shifted(fluxes[1, :, -1:].astype(jnp.bfloat16), "gy", 1).astype(jnp.float32)
    lower_x = jnp.concatenate([edge_x, fluxes[0, :-1]], axis=0)
    lower_y = jnp.concatenate([edge_y, fluxes[1, :, :-1]], axis=1)
    lower_z = jnp.pad(fluxes[2], ((0, 0), (0, 0), (1, 0)))[:, :, :-1]
    source = lower_x - fluxes[0] + (lower_y - fluxes[1]) + (lower_z - fluxes[2])
    screens = [point_counts.astype(jnp.float32) * screen_weight]
    for level_index in range(LEVELS):
        screens.append(restrict(screens[-1]))
    factors = [0.25**level_index for level_index in range(LEVELS + 1)]
    inv_diags = [
        1.0 / (6.0 * factors[level_index] + screens[level_index]) for level_index in range(LEVELS)
    ]

    def vcycle(iterate, target, level_index):
        iterate = smooth(
            iterate,
            target,
            screens[level_index],
            inv_diags[level_index],
            factors[level_index],
            level_index,
        )
        remain = target - operate(iterate, screens[level_index], factors[level_index], level_index)
        coarse_target = restrict(remain)
        if level_index + 1 == LEVELS:
            coarse_error = spread_solve(coarse_target, screens[LEVELS], factors[LEVELS])
        else:
            coarse_error = vcycle(jnp.zeros_like(coarse_target), coarse_target, level_index + 1)
        iterate = iterate + prolong(coarse_error)
        return smooth(
            iterate,
            target,
            screens[level_index],
            inv_diags[level_index],
            factors[level_index],
            level_index,
        )

    solution = jnp.zeros_like(source)
    for cycle_index in range(CYCLES):
        solution = vcycle(solution, source, 0)
    residual = source - operate(solution, screens[0], factors[0], 0)
    return (solution, residual)


def solution(mesh):
    return jax.shard_map(
        per_device,
        mesh=mesh,
        in_specs=(P("gx", "gy", None), P(None, "gx", "gy", None)),
        out_specs=(P("gx", "gy", None), P("gx", "gy", None)),
        check_vma=False,
    )
```

profile of v0, /device:TPU:1, one launch (start us, length us, event | category | flops | bytes accessed | tf_op | source)
XLA Modules:
  0.0 2403.3 jit_solution(14357959046961158328)
XLA Ops:
  31.8 5.1 collective-permute-start.9
  38.2 5.3 collective-permute-start.15
  62.1 9.8 reshape.84
  76.4 9.8 reshape.83
  91.6 5.1 collective-permute-start.19
  104.3 5.7 collective-permute-start.27
  111.6 5.2 collective-permute-start.23
  132.3 5.2 collective-permute-start.31
  146.8 5.4 collective-permute-start.35
  162.4 5.2 collective-permute-start.39
  176.7 93.5 %all-reduce.49 = (f32[]{:T(128)}, f32[]{:T(128)}) all-reduce(f32[]{:T(128)} %get-tuple-element.7, f32[]{:T(128)} %get-tuple-element.6), channel_id=1, replica_groups=mesh['gx'=32,'gy'=8] {'gx','gy'}, use_global_device_ids=true, to_apply=%region_6.7 | all-reduce | flops 2 | bytes 16 | tf_op jit(solution)/shard_map/psum | solution.py:87
  272.2 73.6 %psum.170 = f32[]{:T(128)} all-reduce(f32[]{:T(128)} %multiply_reduce_fusion.19), channel_id=1, replica_groups=mesh['gx'=32,'gy'=8] {'gx','gy'}, use_global_device_ids=true, to_apply=%region_11.12 | all-reduce | flops 1 | bytes 8 | tf_op jit(solution)/shard_map/psum | solution.py:87
  361.2 77.5 %psum.171 = f32[]{:T(128)} all-reduce(f32[]{:T(128)} %get-tuple-element.53), channel_id=1, replica_groups=mesh['gx'=32,'gy'=8] {'gx','gy'}, use_global_device_ids=true, to_apply=%region_13.14 | all-reduce | flops 1 | bytes 8 | tf_op jit(solution)/shard_map/psum | solution.py:97
  440.7 73.4 %psum.172 = f32[]{:T(128)} all-reduce(f32[]{:T(128)} %get-tuple-element.51), channel_id=1, replica_groups=mesh['gx'=32,'gy'=8] {'gx','gy'}, use_global_device_ids=true, to_apply=%region_15.16 | all-reduce | flops 1 | bytes 8 | tf_op jit(solution)/shard_map/psum | solution.py:87
  529.0 77.5 %psum.173 = f32[]{:T(128)} all-reduce(f32[]{:T(128)} %get-tuple-element.49), channel_id=1, replica_groups=mesh['gx'=32,'gy'=8] {'gx','gy'}, use_global_device_ids=true, to_apply=%region_17.18 | all-reduce | flops 1 | bytes 8 | tf_op jit(solution)/shard_map/psum | solution.py:97
  608.5 73.4 %psum.174 = f32[]{:T(128)} all-reduce(f32[]{:T(128)} %get-tuple-element.47), channel_id=1, replica_groups=mesh['gx'=32,'gy'=8] {'gx','gy'}, use_global_device_ids=true, to_apply=%region_19.20 | all-reduce | flops 1 | bytes 8 | tf_op jit(solution)/shard_map/psum | solution.py:87
  696.8 77.5 %psum.175 = f32[]{:T(128)} all-reduce(f32[]{:T(128)} %get-tuple-element.45), channel_id=1, replica_groups=mesh['gx'=32,'gy'=8] {'gx','gy'}, use_global_device_ids=true, to_apply=%region_21.22 | all-reduce | flops 1 | bytes 8 | tf_op jit(solution)/shard_map/psum | solution.py:97
  776.3 73.4 %psum.176 = f32[]{:T(128)} all-reduce(f32[]{:T(128)} %get-tuple-element.43), channel_id=1, replica_groups=mesh['gx'=32,'gy'=8] {'gx','gy'}, use_global_device_ids=true, to_apply=%region_23.24 | all-reduce | flops 1 | bytes 8 | tf_op jit(solution)/shard_map/psum | solution.py:87
  864.6 77.5 %psum.177 = f32[]{:T(128)} all-reduce(f32[]{:T(128)} %get-tuple-element.41), channel_id=1, replica_groups=mesh['gx'=32,'gy'=8] {'gx','gy'}, use_global_device_ids=true, to_apply=%region_25.26 | all-reduce | flops 1 | bytes 8 | tf_op jit(solution)/shard_map/psum | solution.py:97
  944.1 73.4 %psum.178 = f32[]{:T(128)} all-reduce(f32[]{:T(128)} %multiply_reduce_fusion.11), channel_id=1, replica_groups=mesh['gx'=32,'gy'=8] {'gx','gy'}, use_global_device_ids=true, to_apply=%region_27.28 | all-reduce | flops 1 | bytes 8 | tf_op jit(solution)/shard_map/psum | solution.py:87
  1032.5 77.5 %psum.179 = f32[]{:T(128)} all-reduce(f32[]{:T(128)} %fusion.339), channel_id=1, replica_groups=mesh['gx'=32,'gy'=8] {'gx','gy'}, use_global_device_ids=true, to_apply=%region_29.30 | all-reduce | flops 1 | bytes 8 | tf_op jit(solution)/shard_map/psum | solution.py:97
  1162.5 5.3 collective-permute-start.77
  1172.5 6.9 reshape.89
  1203.2 5.0 collective-permute-start.85
  1210.8 5.7 collective-permute-start.87
  1219.3 5.0 collective-permute-start.89
  1226.8 5.7 collective-permute-start.91
  1242.9 5.7 collective-permute-start.95
  1257.6 9.8 reshape.90
  1272.7 5.7 collective-permute-start.99
  1288.5 5.7 collective-permute-start.103
  1305.5 5.7 collective-permute-start.107
  1321.1 5.7 collective-permute-start.111
  1337.0 5.7 collective-permute-start.115
  1352.0 95.4 %all-reduce.48 = (f32[]{:T(128)}, f32[]{:T(128)}) all-reduce(f32[]{:T(128)} %get-tuple-element.5, f32[]{:T(128)} %get-tuple-element.4), channel_id=1, replica_groups=mesh['gx'=32,'gy'=8] {'gx','gy'}, use_global_device_ids=true, to_apply=%region_34.35 | all-reduce | flops 2 | bytes 16 | tf_op jit(solution)/shard_map/psum | solution.py:87
  1449.4 73.4 %psum.182 = f32[]{:T(128)} all-reduce(f32[]{:T(128)} %multiply_reduce_fusion.8), channel_id=1, replica_groups=mesh['gx'=32,'gy'=8] {'gx','gy'}, use_global_device_ids=true, to_apply=%region_38.39 | all-reduce | flops 1 | bytes 8 | tf_op jit(solution)/shard_map/psum | solution.py:87
  1537.7 78.0 %psum.183 = f32[]{:T(128)} all-reduce(f32[]{:T(128)} %get-tuple-element.30), channel_id=1, replica_groups=mesh['gx'=32,'gy'=8] {'gx','gy'}, use_global_device_ids=true, to_apply=%region_40.41 | all-reduce | flops 1 | bytes 8 | tf_op jit(solution)/shard_map/psum | solution.py:97
  1617.6 73.4 %psum.184 = f32[]{:T(128)} all-reduce(f32[]{:T(128)} %get-tuple-element.28), channel_id=1, replica_groups=mesh['gx'=32,'gy'=8] {'gx','gy'}, use_global_device_ids=true, to_apply=%region_42.43 | all-reduce | flops 1 | bytes 8 | tf_op jit(solution)/shard_map/psum | solution.py:87
  1705.9 77.5 %psum.185 = f32[]{:T(128)} all-reduce(f32[]{:T(128)} %get-tuple-element.26), channel_id=1, replica_groups=mesh['gx'=32,'gy'=8] {'gx','gy'}, use_global_device_ids=true, to_apply=%region_44.45 | all-reduce | flops 1 | bytes 8 | tf_op jit(solution)/shard_map/psum | solution.py:97
  1785.4 73.4 %psum.186 = f32[]{:T(128)} all-reduce(f32[]{:T(128)} %get-tuple-element.24), channel_id=1, replica_groups=mesh['gx'=32,'gy'=8] {'gx','gy'}, use_global_device_ids=true, to_apply=%region_46.47 | all-reduce | flops 1 | bytes 8 | tf_op jit(solution)/shard_map/psum | solution.py:87
  1873.8 77.5 %psum.187 = f32[]{:T(128)} all-reduce(f32[]{:T(128)} %get-tuple-element.22), channel_id=1, replica_groups=mesh['gx'=32,'gy'=8] {'gx','gy'}, use_global_device_ids=true, to_apply=%region_48.49 | all-reduce | flops 1 | bytes 8 | tf_op jit(solution)/shard_map/psum | solution.py:97
  1953.2 73.4 %psum.188 = f32[]{:T(128)} all-reduce(f32[]{:T(128)} %get-tuple-element.20), channel_id=1, replica_groups=mesh['gx'=32,'gy'=8] {'gx','gy'}, use_global_device_ids=true, to_apply=%region_50.51 | all-reduce | flops 1 | bytes 8 | tf_op jit(solution)/shard_map/psum | solution.py:87
  2041.6 77.5 %psum.189 = f32[]{:T(128)} all-reduce(f32[]{:T(128)} %get-tuple-element.18), channel_id=1, replica_groups=mesh['gx'=32,'gy'=8] {'gx','gy'}, use_global_device_ids=true, to_apply=%region_52.53 | all-reduce | flops 1 | bytes 8 | tf_op jit(solution)/shard_map/psum | solution.py:97
  2121.1 73.4 %psum.190 = f32[]{:T(128)} all-reduce(f32[]{:T(128)} %multiply_reduce_fusion), channel_id=1, replica_groups=mesh['gx'=32,'gy'=8] {'gx','gy'}, use_global_device_ids=true, to_apply=%region_54.55 | all-reduce | flops 1 | bytes 8 | tf_op jit(solution)/shard_map/psum | solution.py:87
  2209.4 77.5 %psum.191 = f32[]{:T(128)} all-reduce(f32[]{:T(128)} %fusion.340), channel_id=1, replica_groups=mesh['gx'=32,'gy'=8] {'gx','gy'}, use_global_device_ids=true, to_apply=%region_56.57 | all-reduce | flops 1 | bytes 8 | tf_op jit(solution)/shard_map/psum | solution.py:97
  2339.5 5.2 collective-permute-start.153
  2349.4 6.9 reshape.95
  2387.8 5.7 collective-permute-start.163
  (559 shorter events, 513.0 us)
Async XLA Ops:
  0.6 15.1 collective-permute-start.2
  1.9 13.8 collective-permute-start.3
  8.0 13.4 collective-permute-start.1
  12.2 9.3 collective-permute-start
  29.8 13.7 collective-permute-start.8
  31.8 11.8 collective-permute-start.9
  36.9 13.8 collective-permute-start.14
  38.2 12.5 collective-permute-start.15
  44.9 11.5 collective-permute-start.10
  46.2 10.2 collective-permute-start.11
  50.8 11.2 collective-permute-start.16
  52.7 9.3 collective-permute-start.17
  56.4 19.5 collective-permute-start.12
  58.3 17.6 collective-permute-start.13
  97.4 12.6 collective-permute-start.20
  99.4 10.7 collective-permute-start.21
  103.0 13.8 collective-permute-start.26
  104.3 12.5 collective-permute-start.27
  110.3 12.1 collective-permute-start.22
  111.6 10.9 collective-permute-start.23
  116.9 11.2 collective-permute-start.28
  118.8 9.3 collective-permute-start.29
  168.3 7.2 collective-permute-start.40
  1146.1 7.0 collective-permute-start.72
  1160.6 7.2 collective-permute-start.76
  1186.1 7.0 collective-permute-start.80
  1201.3 7.0 collective-permute-start.84
  1209.5 7.1 collective-permute-start.86
  1217.3 7.0 collective-permute-start.88
  1225.5 7.1 collective-permute-start.90
  1233.4 7.0 collective-permute-start.92
  1241.6 7.1 collective-permute-start.94
  1249.4 7.0 collective-permute-start.96
  1271.4 7.1 collective-permute-start.98
  1279.2 7.0 collective-permute-start.100
  1287.2 7.1 collective-permute-start.102
  1295.0 7.0 collective-permute-start.104
  1304.2 7.1 collective-permute-start.106
  1312.0 7.0 collective-permute-start.108
  1319.8 7.1 collective-permute-start.110
  1327.6 7.0 collective-permute-start.112
  1335.7 7.1 collective-permute-start.114
  2323.0 7.0 collective-permute-start.148
  2337.5 7.2 collective-permute-start.152
  2363.0 7.0 collective-permute-start.156
  2378.2 7.0 collective-permute-start.160
  2386.5 7.1 collective-permute-start.162
  2394.3 7.0 collective-permute-start.164
  (120 other events, 672.4 us)
where the time goes:
time: 2430 us; the launch traced here: 2400 us
  blocking collectives  1700 us (70%)
  starting transfers between devices  522 us (21%)
  local copies, waits for them, and re-layouts  56.9 us (2%)
  waiting for transfers between devices  51.8 us (2%)
  other arithmetic  40.1 us (2%)
  between operations  33.4 us (1%)
    psum x12, blocking collectives, squares_total(): return lax.psum(jnp.sum(field * field), ('gx', 'gy'))  923 us
    psum x10, blocking collectives, spread_solve(): step_length = norm_now / lax.psum(jnp.sum(search * image), ('gx', 'gy'))  776 us
    ppermute x82, starting transfers between devices, padded_2(): lax.ppermute(lax.slice_in_dim(block, block.shape[dim] - width, None, axis...  360 us
    ppermute x82, starting transfers between devices, padded_2(): lax.ppermute(lax.slice_in_dim(block, 0, width, axis=dim), axis, backward)  155 us
    ppermute x82, waiting for transfers between devices, padded_2(): lax.ppermute(lax.slice_in_dim(block, block.shape[dim] - width, None, axis...  51.5 us
  transfers between devices with their start and end apart: 166, of which 71 were waited for; matrix products, arithmetic and copies ran while one was open for 1% of the time, Pallas kernels for 0%

commit v1 on v0

v1 whole, which is shorter than its diff:
```python
import functools

import jax
import jax.numpy as jnp
from jax import lax
from jax.experimental import pallas as pl
from jax.experimental.pallas import tpu as pltpu
from jax.sharding import PartitionSpec as P


MESH = pl.DeviceIdType.MESH
F32 = jnp.float32
BF16 = jnp.bfloat16
NEIGH = tuple((dx, dy) for dx in (-1, 0, 1) for dy in (-1, 0, 1) if (dx, dy) != (0, 0))

CENTRE = 0.5 * (2.0 + 0.3)
RADIUS = 0.5 * (2.0 - 0.3)
RATIO = CENTRE / RADIUS
MOM = 1.0 / RATIO
MOM2 = 1.0 / (2.0 * RATIO - MOM)
C1 = 1.0 / CENTRE
CA = MOM2 * MOM
CB = 2.0 * MOM2 / RADIUS
COARSE_ITERS = 6


def lanes(shape):
    return lax.broadcasted_iota(jnp.int32, shape, len(shape) - 1)


def rows(shape):
    return lax.broadcasted_iota(jnp.int32, shape, len(shape) - 2)


def roll(v, shift, axis):
    return pltpu.roll(v, shift, axis)


def zpair(v, width):
    axis = v.ndim - 1
    low = (lanes(v.shape) & width) == 0
    return v + jnp.where(low, roll(v, 128 - width, axis), roll(v, width, axis))


def side_sum(c, up, dn, shift):
    ax = c.ndim - 2
    count = c.shape[ax]
    lane = lanes(c.shape)
    total = up + dn
    total = total + (roll(c, 1, ax) + roll(c, count - 1, ax))
    low = jnp.where(lane < shift, 0.0, roll(c, shift, ax + 1))
    high = jnp.where(lane >= 128 - shift, 0.0, roll(c, 128 - shift, ax + 1))
    return total + (low + high)


def sweep(lo, hi, step, body):
    def one(k, carry):
        body(lo + k * step)
        return carry

    lax.fori_loop(0, (hi - lo) // step, one, 0)


class Level:
    def __init__(self, x, y, d, g, s, inv, depth, step):
        self.x, self.y, self.d, self.g, self.s, self.inv = x, y, d, g, s, inv
        self.shift = 2**depth
        self.factor = 0.25**depth
        self.step = step

    def apply(self, src, i, n):
        c = src[pl.ds(i + 1, n)]
        around = side_sum(c, src[pl.ds(i + 2, n)], src[pl.ds(i, n)], self.shift)
        return c, (6.0 * c - around) * self.factor + self.s[pl.ds(i, n)] * c

    def first_zero(self, lo, hi):
        n = self.step

        def body(i):
            self.x[pl.ds(i + 1, n)] = self.g[pl.ds(i, n)] * self.inv[pl.ds(i, n)] * C1

        sweep(lo, hi, n, body)

    def second_zero(self, lo, hi):
        n = self.step

        def body(i):
            c, image = self.apply(self.x, i, n)
            z = (self.g[pl.ds(i, n)] - image) * self.inv[pl.ds(i, n)]
            self.y[pl.ds(i + 1, n)] = c + (CA * c + CB * z)

        sweep(lo, hi, n, body)

    def pass_one(self, lo, hi):
        n = self.step

        def body(i):
            c, image = self.apply(self.y, i, n)
            d = (self.g[pl.ds(i, n)] - image) * self.inv[pl.ds(i, n)] * C1
            self.d[pl.ds(i, n)] = d
            self.x[pl.ds(i + 1, n)] = c + d

        sweep(lo, hi, n, body)

    def pass_two(self, lo, hi):
        n = self.step

        def body(i):
            c, image = self.apply(self.x, i, n)
            z = (self.g[pl.ds(i, n)] - image) * self.inv[pl.ds(i, n)]
            self.y[pl.ds(i + 1, n)] = c + (CA * self.d[pl.ds(i, n)] + CB * z)

        sweep(lo, hi, n, body)

    def residual(self, lo, hi, store):
        n = self.step

        def body(i):
            _, image = self.apply(self.y, i, n)
            store(i, n, self.g[pl.ds(i, n)] - image)

        sweep(lo, hi, n, body)


def scratch_list(ngx):
    v = pltpu.VMEM
    return (
        ("fcv", v((3, 16, 16, 128), jnp.int32)),
        ("pcv", v((16, 16, 128), jnp.int32)),
        ("ext", v((32, 4, 16, 128), BF16)),
        ("exs", v((2, 16, 128), BF16)),
        ("rex", v((8, 2, 16, 128), BF16)),
        ("s1p", v((4, 16, 128), BF16)),
        ("rs1", v((8, 4, 16, 128), BF16)),
        ("scrown", v((16, 16, 128), F32)),
        ("s1own", v((8, 8, 128), F32)),
        ("fy1", v((32, 128), F32)),
        ("fy2", v((32, 128), F32)),
        ("x0", v((34, 32, 128), F32)),
        ("y0", v((34, 32, 128), F32)),
        ("d0", v((32, 32, 128), F32)),
        ("g0", v((32, 32, 128), F32)),
        ("s0", v((32, 32, 128), F32)),
        ("i0", v((32, 32, 128), F32)),
        ("r0", v((16, 16, 128), F32)),
        ("pe0", v((16, 32, 128), F32)),
        ("pk", v((2, 4, 8, 128), F32)),
        ("rb", v((2, 8, 4, 8, 128), F32)),
        ("x1", v((26, 24, 128), F32)),
        ("y1", v((26, 24, 128), F32)),
        ("d1", v((24, 24, 128), F32)),
        ("g1", v((24, 24, 128), F32)),
        ("s1", v((24, 24, 128), F32)),
        ("i1", v((24, 24, 128), F32)),
        ("r1", v((16, 24, 128), F32)),
        ("pe1", v((16, 24, 128), F32)),
        ("s2t", v((8, 8, 128), F32)),
        ("i2t", v((8, 8, 128), F32)),
        ("rs2", v((8, 8, 8, 128), F32)),
        ("g2t", v((2, 8, 8, 128), F32)),
        ("rg2", v((2, 8, 8, 8, 128), F32)),
        ("x2", v((18, 16, 128), F32)),
        ("y2", v((18, 16, 128), F32)),
        ("d2", v((16, 16, 128), F32)),
        ("g2", v((16, 16, 128), F32)),
        ("s2", v((16, 16, 128), F32)),
        ("i2", v((16, 16, 128), F32)),
        ("pe2", v((8, 16, 128), F32)),
        ("tile", v((3, 8, 128), F32)),
        ("p1", v((3, 7, 8, 128), F32)),
        ("agb", v((3, ngx, 8, 128), F32)),
        ("s3", v((ngx // 2, 8, 128), F32)),
        ("e3", v((ngx // 2, 8, 128), F32)),
        ("snd", pltpu.SemaphoreType.DMA((8, 8))),
        ("rcv", pltpu.SemaphoreType.DMA((8, 8))),
        ("ags", pltpu.SemaphoreType.DMA((3, 4))),
        ("loc", pltpu.SemaphoreType.DMA((2,))),
    )


EX_IN, EX_FACE, EX_S1, EX_S2, EX_B, EX_G = 0, 1, 2, 3, 4, 6


def kernel(ngx, ngy, names, pc_hbm, fc_hbm, sol_ref, res_ref, *scratch):
    m = dict(zip(names, scratch))
    gx = lax.axis_index("gx")
    gy = lax.axis_index("gy")
    half = ngx // 2
    nx0, ny0 = 16 * ngx, 16 * ngy

    def wrap_x(v):
        return lax.rem(v + ngx, ngx)

    def wrap_y(v):
        return lax.rem(v + ngy, ngy)

    copy_p = pltpu.make_async_copy(pc_hbm, m["pcv"], m["loc"].at[0])
    copy_f = pltpu.make_async_copy(fc_hbm, m["fcv"], m["loc"].at[1])
    copy_p.start()
    copy_f.start()

    barrier = pltpu.get_barrier_semaphore()
    peers = 0
    for o in range(1, ngy):
        pl.semaphore_signal(barrier, inc=1, device_id=(gx, wrap_y(gy + o)), device_id_type=MESH)
        peers += 1

    def greet(o, carry):
        pl.semaphore_signal(barrier, inc=1, device_id=(wrap_x(gx + o), gy), device_id_type=MESH)
        return carry

    lax.fori_loop(1, ngx, greet, 0)
    peers += ngx - 1
    for dx, dy in NEIGH:
        if dx != 0 and dy != 0:
            pl.semaphore_signal(
                barrier, inc=1, device_id=(wrap_x(gx + dx), wrap_y(gy + dy)), device_id_type=MESH
            )
            peers += 1

    for name in ("x0", "y0", "x1", "y1", "x2", "y2"):
        ref = m[name]
        last = ref.shape[0] - 1
        ref[0] = jnp.zeros(ref.shape[1:], F32)
        ref[last] = jnp.zeros(ref.shape[1:], F32)

    copy_p.wait()
    copy_f.wait()
    fcv, pcv = m["fcv"], m["pcv"]

    def own_row(i):
        f0 = fcv[0, i].astype(F32) * 0.125
        before = fcv[0, jnp.maximum(i - 1, 0)].astype(F32) * 0.125
        f1 = fcv[1, i].astype(F32) * 0.125
        f2 = fcv[2, i].astype(F32) * 0.125
        low_x = jnp.where(i > 0, before, 0.0)
        low_y = jnp.where(rows(f1.shape) == 0, 0.0, roll(f1, 1, 0))
        low_z = jnp.where(lanes(f2.shape) == 0, 0.0, roll(f2, 1, 1))
        src = (low_x - f0) + (low_y - f1) + (low_z - f2)
        scr = pcv[i].astype(F32) * 0.25
        m["scrown"][i] = scr
        for t in range(2):
            part = slice(8 * t, 8 * t + 8)
            m["ext"][i + 8, t + 1] = jnp.concatenate([src[part], scr[part]], axis=0).astype(BF16)

    sweep(0, 16, 1, own_row)

    tile_shape = (8, 128)
    sub = rows(tile_shape)
    lane = lanes(tile_shape)
    face_x = fcv[0, 15].astype(F32) * 0.125
    own_fx = [face_x[0:8], face_x[8:16]]
    own_fy = []
    for h in range(2):
        total = jnp.zeros(tile_shape, F32)
        for r in range(8):
            row = fcv[1, 8 * h + r, 15:16].astype(F32) * 0.125
            total = jnp.where(sub == r, row, total)
        own_fy.append(total)
    for t in range(2):
        m["exs"][t] = jnp.concatenate([own_fx[t], own_fy[t]], axis=0).astype(BF16)

    own1 = []
    for i in range(8):
        total = jnp.zeros(tile_shape, F32)
        for q in range(2):
            for j in range(2):
                total = total + m["scrown"][2 * i + q, pl.ds(j, 8, stride=2), :]
        v = zpair(total, 1) * 0.125
        m["s1own"][i] = v
        own1.append(v)
    for k in range(4):
        m["s1p"][k] = jnp.concatenate([own1[2 * k], own1[2 * k + 1]], axis=0).astype(BF16)

    def pack3(parts):
        slot = lane & 3
        total = jnp.zeros(tile_shape, F32)
        for xi in range(2):
            for yi in range(2):
                total = jnp.where(slot == 2 * xi + yi, parts[xi][yi], total)
        return total

    own3 = []
    for xi in range(2):
        pair = jnp.zeros((4, 128), F32)
        for q in range(2):
            quad = jnp.zeros((4, 128), F32)
            for h in range(2):
                for j in range(2):
                    quad = quad + m["s1own"][4 * xi + 2 * q + h, pl.ds(j, 4, stride=2), :]
            pair = pair + zpair(quad, 2) * 0.125
        pair = zpair(pair, 4) * 0.125
        own3.append([pair[0:1] + pair[1:2], pair[2:3] + pair[3:4]])
    m["tile"][2] = pack3(own3)

    pl.semaphore_wait(barrier, peers)

    sent = []

    def exchange(kind, make):
        copies = []
        for n, (dx, dy) in enumerate(NEIGH):
            src, dst = make(n, dx, dy)
            copy = pltpu.make_async_remote_copy(
                src_ref=src,
                dst_ref=dst,
                send_sem=m["snd"].at[kind, n],
                recv_sem=m["rcv"].at[kind, n],
                device_id=(wrap_x(gx + dx), wrap_y(gy + dy)),
                device_id_type=MESH,
            )
            copy.start()
            copies.append(copy)
        sent.extend(copies)
        return copies

    def arrive(copies):
        for copy in copies:
            copy.wait_recv()

    def from_source(px, py):
        return NEIGH.index((-px, -py))

    spans = {1: (8, 8, 0), 0: (0, 16, 8), -1: (0, 8, 24)}
    tiles = {1: (1, 1, 0), 0: (0, 2, 1), -1: (0, 1, 3)}

    def make_in(n, dx, dy):
        xs, xn, xd = spans[dx]
        ys, yn, yd = tiles[dy]
        src = m["ext"].at[pl.ds(xs + 8, xn), pl.ds(ys + 1, yn)]
        dst = m["ext"].at[pl.ds(xd, xn), pl.ds(yd, yn)]
        return src, dst

    copies_face = exchange(EX_FACE, lambda n, dx, dy: (m["exs"], m["rex"].at[n]))
    copies_in = exchange(EX_IN, make_in)
    copies_s1 = exchange(EX_S1, lambda n, dx, dy: (m["s1p"], m["rs1"].at[n]))

    def gather_one(c):
        for o in range(1, ngy):
            pltpu.make_async_remote_copy(
                src_ref=m["tile"].at[c],
                dst_ref=m["p1"].at[c, o - 1],
                send_sem=m["ags"].at[c, 0],
                recv_sem=m["ags"].at[c, 1],
                device_id=(gx, wrap_y(gy + o)),
                device_id_type=MESH,
            ).start()

    def wait_bytes(ref, sem):
        pltpu.make_async_copy(ref, ref, sem).wait()

    def gather_two(c):
        wait_bytes(m["p1"].at[c, pl.ds(0, ngy - 1)], m["ags"].at[c, 1])
        total = jnp.where(sub == gy, m["tile"][c], 0.0)
        for o in range(1, ngy):
            total = jnp.where(sub == wrap_y(gy - o), m["p1"][c, o - 1], total)
        m["agb"][c, gx] = total

        def send(o, carry):
            pltpu.make_async_remote_copy(
                src_ref=m["agb"].at[c, gx],
                dst_ref=m["agb"].at[c, gx],
                send_sem=m["ags"].at[c, 2],
                recv_sem=m["ags"].at[c, 3],
                device_id=(wrap_x(gx + o), gy),
                device_id_type=MESH,
            ).start()
            return carry

        lax.fori_loop(1, ngx, send, 0)

    def gather_done(c):
        wait_bytes(m["agb"].at[c, pl.ds(0, ngx - 1)], m["ags"].at[c, 3])
        full = (half, 8, 128)
        return jnp.where((lanes(full) & 4) == 0, m["agb"][c, 0:half], m["agb"][c, half:ngx])

    gather_one(2)

    arrive(copies_face)
    gate_x = jnp.where(gx > 0, 1.0, 0.0)
    gate_y = jnp.where(gy > 0, 1.0, 0.0)

    def face(px, py, t):
        return m["rex"][from_source(px, py), t].astype(F32)

    m["fy1"][0:8] = face(-1, -1, 1)[8:16] * gate_y
    m["fy1"][8:16] = face(0, -1, 0)[8:16] * gate_y
    m["fy1"][16:24] = face(0, -1, 1)[8:16] * gate_y
    m["fy1"][24:32] = face(1, -1, 0)[8:16] * gate_y
    m["fy2"][0:8] = face(-1, 0, 1)[8:16]
    m["fy2"][8:16] = own_fy[0]
    m["fy2"][16:24] = own_fy[1]
    m["fy2"][24:32] = face(1, 0, 0)[8:16]
    arrive(copies_in)

    def inside(shape, i, level, off_x, off_y):
        x = lax.broadcasted_iota(jnp.int32, shape, 0) + (i - off_x + gx * (16 >> level))
        y = rows(shape) + (gy * (16 >> level) - off_y)
        return (x >= 0) & (x < (nx0 >> level)) & (y >= 0) & (y < (ny0 >> level))

    def inverse(scr, i, level, off):
        mask = inside(scr.shape, i, level, off, off)
        return jnp.where(mask, 1.0 / (6.0 * 0.25**level + scr), 0.0)

    def unpack_in(i):
        for t in range(4):
            pair = m["ext"][i, t].astype(F32)
            src = pair[0:8]
            if t == 1:
                src = src + jnp.where(sub == 0, m["fy1"][pl.ds(i, 1)], 0.0)
            if t == 3:
                src = src + jnp.where(sub == 0, m["fy2"][pl.ds(i, 1)], 0.0)
            m["g0"][i, 8 * t : 8 * t + 8] = src
            m["s0"][i, 8 * t : 8 * t + 8] = pair[8:16]

    sweep(0, 32, 1, unpack_in)
    for t, (py, k) in enumerate(((-1, 1), (0, 0), (0, 1), (1, 0))):
        part = slice(8 * t, 8 * t + 8)
        m["g0"][8, part] = m["g0"][8, part] + face(-1, py, k)[0:8] * gate_x
        upper = own_fx[k] if py == 0 else face(0, py, k)[0:8]
        m["g0"][24, part] = m["g0"][24, part] + upper

    lv0 = Level(m["x0"], m["y0"], m["d0"], m["g0"], m["s0"], m["i0"], 0, 4)
    lv1 = Level(m["x1"], m["y1"], m["d1"], m["g1"], m["s1"], m["i1"], 1, 4)
    lv2 = Level(m["x2"], m["y2"], m["d2"], m["g2"], m["s2"], m["i2"], 2, 8)

    def make_inv(level, step, count, off):
        def body(i):
            level.inv[pl.ds(i, step)] = inverse(level.s[pl.ds(i, step)], i, level.shift.bit_length() - 1, off)

        sweep(0, count, step, body)

    make_inv(lv0, 4, 32, 8)

    odd = (lane & 1) == 1
    copies_b = [None, None]
    copies_g = [None, None]

    def send_b(c):
        def store(i, n, r):
            m["r0"][pl.ds(i - 8, n)] = r[:, 8:24]

        lv0.residual(8, 24, store)
        fine = []
        for i in range(8):
            total = jnp.zeros(tile_shape, F32)
            for q in range(2):
                for j in range(2):
                    total = total + m["r0"][2 * i + q, pl.ds(j, 8, stride=2), :]
            v = zpair(total, 1) * 0.125
            m["g1"][8 + i, 8:16] = v
            fine.append(v)
        for k in range(4):
            m["pk"][c, k] = jnp.where(odd, fine[2 * k + 1], fine[2 * k])
        copies_b[c] = exchange(EX_B + c, lambda n, dx, dy: (m["pk"].at[c], m["rb"].at[c, n]))

    def take_b(c):
        arrive(copies_b[c])
        for n, (dx, dy) in enumerate(NEIGH):
            base = 8 - 8 * dx
            part = slice(8 - 8 * dy, 16 - 8 * dy)
            for k in range(4):
                v = m["rb"][c, n, k]
                m["g1"][base + 2 * k, part] = jnp.where(odd, roll(v, 1, 1), v)
                m["g1"][base + 2 * k + 1, part] = jnp.where(odd, v, roll(v, 127, 1))

    def setup_level1():
        arrive(copies_s1)
        for i in range(8):
            m["s1"][8 + i, 8:16] = m["s1own"][i]
        for n, (dx, dy) in enumerate(NEIGH):
            base = 8 - 8 * dx
            part = slice(8 - 8 * dy, 16 - 8 * dy)
            for k in range(4):
                v = m["rs1"][n, k].astype(F32)
                m["s1"][base + 2 * k, part] = v[0:8]
                m["s1"][base + 2 * k + 1, part] = v[8:16]
        make_inv(lv1, 4, 24, 8)
        for i in range(8):
            total = jnp.zeros(tile_shape, F32)
            for q in range(2):
                for j in range(2):
                    total = total + m["s1"][4 + 2 * i + q, pl.ds(4 + j, 8, stride=2), :]
            m["s2t"][i] = zpair(total, 2) * 0.125
        m["i2t"][...] = inverse(m["s2t"][...], 0, 2, 2)

    def exchange_tile(kind, src, dst):
        def make(n, dx, dy):
            part = {1: pl.ds(0, 4), 0: pl.ds(0, 8), -1: pl.ds(4, 4)}[dx]
            return src.at[part], dst.at[n, part]

        return exchange(kind, make)

    def assemble(own, got, out):
        for i in range(16):
            px = -1 if i < 4 else (0 if i < 12 else 1)
            r = i - 4 * px - 4
            for py, part in ((-1, slice(0, 8)), (1, slice(8, 16)), (0, slice(4, 12))):
                out[i, part] = own[r] if (px, py) == (0, 0) else got[from_source(px, py), r]

    def pre_level1(c):
        lv1.first_zero(0, 24)
        lv1.second_zero(0, 24)

        def store(i, n, r):
            m["r1"][pl.ds(i - 4, n)] = r

        lv1.residual(4, 20, store)
        small = []
        for i in range(8):
            total = jnp.zeros(tile_shape, F32)
            for q in range(2):
                for j in range(2):
                    total = total + m["r1"][2 * i + q, pl.ds(4 + j, 8, stride=2), :]
            small.append((zpair(total, 2) * 0.125)[None])
        g = jnp.concatenate(small, axis=0)
        m["g2t"][c] = g
        scr = m["s2t"][...]
        inv = m["i2t"][...]
        zero = jnp.zeros((1, 8, 128), F32)

        def image(v):
            up = jnp.concatenate([v[1:], zero], axis=0)
            dn = jnp.concatenate([zero, v[:-1]], axis=0)
            return (6.0 * v - side_sum(v, up, dn, 4)) * 0.0625 + scr * v

        v = g * inv * C1
        v = v + (CA * v + CB * ((g - image(v)) * inv))
        r = g - image(v)
        parts = []
        for xi in range(2):
            t = r[2 + 2 * xi] + r[3 + 2 * xi]
            t = zpair(t + roll(t, 7, 0), 4) * 0.125
            parts.append([t[2:3], t[4:5]])
        m["tile"][c] = pack3(parts)

    def dot(a, b):
        t = jnp.sum(a * b, axis=0)
        t = jnp.sum(t, axis=0, keepdims=True)
        return jnp.sum(t, axis=1, keepdims=True)[None]

    full = (half, 8, 128)
    lane3 = lanes(full)
    sub3 = rows(full)

    def image3(f, scr):
        left = roll(f, 126, 2)
        right = roll(f, 2, 2)
        after = jnp.where((lane & 4) == 0, left[0], 0.0)[None]
        ahead = jnp.where((lane & 4) != 0, right[half - 1], 0.0)[None]
        nxt = jnp.concatenate([right[1:], after], axis=0)
        prv = jnp.concatenate([ahead, left[:-1]], axis=0)
        total = jnp.where((lane3 & 2) == 0, left + prv, right + nxt)
        near = roll(f, 127, 2)
        far = roll(f, 1, 2)
        up = jnp.where(sub3 > 0, roll(near, 1, 1), 0.0)
        dn = jnp.where(sub3 < ngy - 1, roll(far, 7, 1), 0.0)
        total = total + jnp.where((lane3 & 1) == 0, near + up, far + dn)
        total = total + jnp.where(lane3 < 8, 0.0, roll(f, 8, 2))
        total = total + jnp.where(lane3 >= 120, 0.0, roll(f, 120, 2))
        q = (6.0 * f - total) * 0.015625 + scr * f
        return q if ngy == 8 else jnp.where(sub3 < ngy, q, 0.0)

    def coarse(g):
        scr = m["s3"][...]
        x = jnp.zeros(full, F32)
        r, p = g, g
        rr = dot(r, r)
        for it in range(COARSE_ITERS):
            q = image3(p, scr)
            alpha = rr / dot(p, q)
            x = x + alpha * p
            if it + 1 < COARSE_ITERS:
                r = r - alpha * q
                new = dot(r, r)
                p = r + (new / rr) * p
                rr = new
        m["e3"][...] = x

    first = (lane & 7) == 0

    def spread(v):
        v = jnp.where(first, v, 0.0)
        v = v + roll(v, 1, 1)
        v = v + roll(v, 2, 1)
        return v + roll(v, 4, 1)

    def post_level2():
        for a in range(-2, 3):
            at = wrap_x(gx + a)
            b = at // half
            t = m["e3"][at - b * half]
            t = roll(t, lax.rem(10 - gy, 8), 0)
            for xi in range(2):
                k = 2 * a + xi + 3
                if not 0 <= k < 8:
                    continue
                u = roll(t, 128 - 2 * xi - 4 * b, 1) if xi else roll(t, lax.rem(128 - 4 * b, 128), 1)
                even = spread(u)[1:5]
                odd_ = spread(roll(u, 127, 1))[0:4]
                m["pe2"][k, pl.ds(0, 4, stride=4), :] = odd_
                m["pe2"][k, pl.ds(1, 4, stride=4), :] = odd_
                m["pe2"][k, pl.ds(2, 4, stride=4), :] = even
                m["pe2"][k, pl.ds(3, 4, stride=4), :] = even
        for i in range(16):
            m["y2"][i + 1] = m["y2"][i + 1] + jnp.where(m["i2"][i] != 0.0, m["pe2"][i // 2], 0.0)
        lv2.pass_one(0, 16)
        lv2.pass_two(0, 16)

    def post_level1(c):
        for k in range(3, 13):
            e = m["y2"][k + 1, 2:14]
            m["pe1"][k, pl.ds(0, 12, stride=2), :] = e
            m["pe1"][k, pl.ds(1, 12, stride=2), :] = e
        lo, hi = ((2, 22), (4, 20))[c]

        def add(k):
            e = m["pe1"][k + 2]
            for q in range(2):
                m["y1"][2 * k + q + 1] = m["y1"][2 * k + q + 1] + e

        sweep(lo // 2, hi // 2, 1, add)
        lv1.pass_one(lo, hi)
        if c == 0:
            lv1.pass_two(4, 20)
        else:
            lv1.pass_two(6, 18)

    def post_level0(c):
        lo, hi = ((0, 32), (4, 28))[c]

        def build(k):
            e = m["y1"][k + 5, 4:20]
            m["pe0"][k, pl.ds(0, 16, stride=2), :] = e
            m["pe0"][k, pl.ds(1, 16, stride=2), :] = e

        def add(k):
            e = m["pe0"][k]
            for q in range(2):
                m["y0"][2 * k + q + 1] = m["y0"][2 * k + q + 1] + e

        sweep(lo // 2, hi // 2, 1, build)
        sweep(lo // 2, hi // 2, 1, add)
        lv0.pass_one(lo, hi)
        if c == 0:
            lv0.pass_two(2, 30)
        else:
            lv0.pass_two(lo, hi)

    for c in range(2):
        if c == 0:
            lv0.first_zero(0, 32)
            lv0.second_zero(0, 32)
        else:
            lv0.pass_one(4, 28)
            lv0.pass_two(4, 28)
        send_b(c)
        if c == 0:
            gather_two(2)
            setup_level1()
            copies_s2 = exchange_tile(EX_S2, m["s2t"], m["rs2"])
        take_b(c)
        pre_level1(c)
        gather_one(c)
        copies_g[c] = exchange_tile(EX_G + c, m["g2t"].at[c], m["rg2"].at[c])
        if c == 0:
            arrive(copies_s2)
            assemble(m["s2t"], m["rs2"], m["s2"])
            make_inv(lv2, 8, 16, 6)
        gather_two(c)
        arrive(copies_g[c])
        assemble(m["g2t"].at[c], m["rg2"].at[c], m["g2"])
        lv2.first_zero(0, 16)
        lv2.second_zero(0, 16)
        if c == 0:
            m["s3"][...] = gather_done(2)
        coarse(gather_done(c))
        post_level2()
        post_level1(c)
        post_level0(c)

    def store(i, n, r):
        res_ref[pl.ds(i - 8, n)] = r[:, 8:24]
        sol_ref[pl.ds(i - 8, n)] = m["y0"][pl.ds(i + 1, n), 8:24]

    lv0.residual(8, 24, store)

    for copy in sent:
        copy.wait_send()
    for c in range(3):
        wait_bytes(m["p1"].at[c, pl.ds(0, ngy - 1)], m["ags"].at[c, 0])
        wait_bytes(m["agb"].at[c, pl.ds(0, ngx - 1)], m["ags"].at[c, 2])


def solution(mesh):
    ngx, ngy = mesh.shape["gx"], mesh.shape["gy"]
    items = scratch_list(ngx)
    names = tuple(name for name, _ in items)

    def per_device(point_counts, face_counts):
        shape = jax.ShapeDtypeStruct(point_counts.shape, F32)
        return pl.pallas_call(
            functools.partial(kernel, ngx, ngy, names),
            out_shape=(shape, shape),
            in_specs=[pl.BlockSpec(memory_space=pl.ANY)] * 2,
            out_specs=(pl.BlockSpec(memory_space=pltpu.VMEM),) * 2,
            scratch_shapes=[spec for _, spec in items],
            compiler_params=pltpu.CompilerParams(
                collective_id=0, has_side_effects=True, vmem_limit_bytes=48 * 1024 * 1024
            ),
            name="poisson",
        )(point_counts, face_counts)

    return jax.shard_map(
        per_device,
        mesh=mesh,
        in_specs=(P("gx", "gy", None), P(None, "gx", "gy", None)),
        out_specs=(P("gx", "gy", None), P("gx", "gy", None)),
        check_vma=False,
    )
```

time: 2430 us -> 72.2 us (0.03); the launches traced: 2400 us -> 72.1 us
  blocking collectives: 1700 us -> 0 us
  starting transfers between devices: 522 us -> 0 us
  Pallas kernels: 0 us -> 68.3 us
  local copies, waits for them, and re-layouts: 56.9 us -> 3.21 us
  waiting for transfers between devices: 51.8 us -> 0 us
  other arithmetic: 40.1 us -> 0 us
  between operations: 33.4 us -> 0.65 us
    psum x22 -> x0, blocking collectives: 1700 us -> none  [the longest x12 923 us: squares_total(): return lax.psum(jnp.sum(field * field), ('gx', 'gy'))]
    ppermute x166 -> x0, starting transfers between devices: 522 us -> none  [the longest x82 360 us: padded_2(): lax.ppermute(lax.slice_in_dim(block, block.shape[dim] - width, None, axis...]
    pallas_call x0 -> x1, Pallas kernels: none -> 68.3 us  [per_device(): pl.pallas_call(functools.partial(kernel, ngx, ngy, names), out_shape=(sha...]
    ppermute x166 -> x0, waiting for transfers between devices: 51.8 us -> none  [the longest x82 51.5 us: padded_2(): lax.ppermute(lax.slice_in_dim(block, block.shape[dim] - width, None, axis...]
    reshape x13 -> x0, local copies, waits for them, and re-layouts: 47 us -> none  [the longest x7 31.7 us: restrict(): blocks = field.reshape(size_x // 2, 2, size_y // 2, 2, size_z // 2, 2)]
    reduce_sum x31 -> x0, other arithmetic: 27.1 us -> none  [the longest x9 12.8 us: restrict(): return blocks.sum(axis=(1, 3, 5)) * 0.125]
  transfers between devices with their start and end apart: 166 -> 0, of which waited for: 71 -> 0; matrix products, arithmetic and copies ran while one was open for 1% -> 0% of each run, Pallas kernels for 0% -> 0%
where the time goes in v1:
time: 72.2 us; the launch traced here: 72.1 us
  Pallas kernels  68.3 us (95%)
  local copies, waits for them, and re-layouts  3.21 us (4%)
    pallas_call x1, Pallas kernels, per_device(): pl.pallas_call(functools.partial(kernel, ngx, ngy, names), out_shape=(sha...  68.3 us
    unnamed x6, local copies, waits for them, and re-layouts  3.21 us

profile of v1, /device:TPU:1, one launch (start us, length us, event | category | flops | bytes accessed | tf_op | source)
XLA Modules:
  0.0 72.1 jit_solution(11552415470239984033)
XLA Ops:
  0.6 0.0 copy-start
  0.6 1.0 %copy-done = s32[3,16,16,128]{3,2,1,0:T(8,128)S(1)} copy-done((s32[3,16,16,128]{3,2,1,0:T(8,128)S(1)}, s32[3,16,16,128]{3,2,1,0:T(8,128)}, u32[]{:S(2)}) %copy-start) | copy-done | bytes 393240
  1.6 0.0 copy-start.1
  1.6 0.9 %copy-done.1 = s32[16,16,128]{2,1,0:T(8,128)S(1)} copy-done((s32[16,16,128]{2,1,0:T(8,128)S(1)}, s32[16,16,128]{2,1,0:T(8,128)}, u32[]{:S(2)}) %copy-start.1) | copy-done | bytes 131096
  2.5 68.3 %poisson.1 = (f32[16,16,128]{2,1,0:T(8,128)S(1)}, f32[16,16,128]{2,1,0:T(8,128)S(1)}) custom-call(s32[16,16,128]{2,1,0:T(8,128)S(1)} %copy-done.1, s32[3,16,16,128]{3,2,1,0:T(8,128)S(1)} %copy-done), custom_call_target="tpu_custom_call" | custom-call | tf_op jit(solution)/shard_map/poisson/pallas_call | solution.py:702
  70.8 0.7 copy.6
  71.5 0.7 copy.7
Async XLA Ops:
  0.6 1.0 %copy-start = (s32[3,16,16,128]{3,2,1,0:T(8,128)S(1)}, s32[3,16,16,128]{3,2,1,0:T(8,128)}, u32[]{:S(2)}) copy-start(s32[3,16,16,128]{3,2,1,0:T(8,128)} %fc_hbm.1) | copy-start | bytes 1179652
  1.6 0.9 %copy-start.1 = (s32[16,16,128]{2,1,0:T(8,128)S(1)}, s32[16,16,128]{2,1,0:T(8,128)}, u32[]{:S(2)}) copy-start(s32[16,16,128]{2,1,0:T(8,128)} %pc_hbm.1) | copy-start | bytes 393220

commit v2 on v1

v2 whole, which is shorter than its diff:
```python
import functools

import jax
import jax.numpy as jnp
from jax import lax
from jax.experimental import pallas as pl
from jax.experimental.pallas import tpu as pltpu
from jax.sharding import PartitionSpec as P


MESH = pl.DeviceIdType.MESH
F32 = jnp.float32
BF16 = jnp.bfloat16
NEIGH = ((-1, -1), (-1, 1), (1, -1), (1, 1), (-1, 0), (1, 0), (0, -1), (0, 1))

CENTRE = 0.5 * (2.0 + 0.3)
RADIUS = 0.5 * (2.0 - 0.3)
RATIO = CENTRE / RADIUS
MOM = 1.0 / RATIO
MOM2 = 1.0 / (2.0 * RATIO - MOM)
C1 = 1.0 / CENTRE
CA = MOM2 * MOM
CB = 2.0 * MOM2 / RADIUS
K0 = 1.0 - C1
K1 = 1.0 + CA - CB
K2 = CB / C1
COARSE_ITERS = 6


def lanes(shape):
    return lax.broadcasted_iota(jnp.int32, shape, len(shape) - 1)


def rows(shape):
    return lax.broadcasted_iota(jnp.int32, shape, len(shape) - 2)


def roll(v, shift, axis):
    return pltpu.roll(v, shift, axis)


def zpair(v, width):
    axis = v.ndim - 1
    low = (lanes(v.shape) & width) == 0
    return v + jnp.where(low, roll(v, 128 - width, axis), roll(v, width, axis))


def side_sum(c, up, dn, shift):
    ax = c.ndim - 2
    count = c.shape[ax]
    lane = lanes(c.shape)
    total = up + dn
    total = total + (roll(c, 1, ax) + roll(c, count - 1, ax))
    low = jnp.where(lane < shift, 0.0, roll(c, shift, ax + 1))
    high = jnp.where(lane >= 128 - shift, 0.0, roll(c, 128 - shift, ax + 1))
    return total + (low + high)


def sweep(lo, hi, step, body):
    def one(k, carry):
        body(lo + k * step)
        return carry

    lax.fori_loop(0, (hi - lo) // step, one, 0)


class Level:
    def __init__(self, x, y, g, w, dg, depth, step):
        self.x, self.y, self.g, self.w, self.dg = x, y, g, w, dg
        self.depth = depth
        self.shift = 2**depth
        self.step = step

    def around(self, src, i, n):
        c = src[pl.ds(i + 1, n)]
        total = side_sum(c, src[pl.ds(i + 2, n)], src[pl.ds(i, n)], self.shift)
        return c, total + self.g[pl.ds(i, n)]

    def first_zero(self, lo, hi):
        n = self.step

        def body(i):
            self.x[pl.ds(i + 1, n)] = self.g[pl.ds(i, n)] * self.w[pl.ds(i, n)]

        sweep(lo, hi, n, body)

    def second_zero(self, lo, hi):
        n = self.step

        def body(i):
            c, t = self.around(self.x, i, n)
            self.y[pl.ds(i + 1, n)] = K1 * c + K2 * (t * self.w[pl.ds(i, n)])

        sweep(lo, hi, n, body)

    def pass_one(self, lo, hi):
        n = self.step

        def body(i):
            c, t = self.around(self.y, i, n)
            self.x[pl.ds(i + 1, n)] = K0 * c + t * self.w[pl.ds(i, n)]

        sweep(lo, hi, n, body)

    def pass_two(self, lo, hi):
        n = self.step

        def body(i):
            c, t = self.around(self.x, i, n)
            old = self.y[pl.ds(i + 1, n)]
            self.y[pl.ds(i + 1, n)] = (K1 * c - CA * old) + K2 * (t * self.w[pl.ds(i, n)])

        sweep(lo, hi, n, body)

    def residual(self, lo, hi, store):
        n = self.step

        def body(i):
            c, t = self.around(self.y, i, n)
            store(i, n, t - self.dg[pl.ds(i, n)] * c)

        sweep(lo, hi, n, body)


def scratch_list(ngx):
    v = pltpu.VMEM
    return (
        ("fcv", v((3, 16, 16, 128), jnp.int32)),
        ("pcv", v((16, 16, 128), jnp.int32)),
        ("ext", v((32, 4, 16, 128), BF16)),
        ("exs", v((2, 16, 128), BF16)),
        ("rex", v((8, 2, 16, 128), BF16)),
        ("s1p", v((4, 16, 128), BF16)),
        ("rs1", v((8, 4, 16, 128), BF16)),
        ("scrown", v((16, 16, 128), F32)),
        ("s1own", v((8, 8, 128), F32)),
        ("fy1", v((32, 128), F32)),
        ("fy2", v((32, 128), F32)),
        ("x0", v((34, 32, 128), F32)),
        ("y0", v((34, 32, 128), F32)),
        ("g0", v((32, 32, 128), F32)),
        ("w0", v((32, 32, 128), F32)),
        ("dg0", v((32, 32, 128), F32)),
        ("r0", v((16, 16, 128), F32)),
        ("pk", v((2, 4, 8, 128), F32)),
        ("rb", v((2, 8, 4, 8, 128), F32)),
        ("x1", v((26, 24, 128), F32)),
        ("y1", v((26, 24, 128), F32)),
        ("g1", v((24, 24, 128), F32)),
        ("s1", v((24, 24, 128), F32)),
        ("w1", v((24, 24, 128), F32)),
        ("dg1", v((24, 24, 128), F32)),
        ("r1", v((16, 24, 128), F32)),
        ("s2t", v((8, 8, 128), F32)),
        ("w2t", v((8, 8, 128), F32)),
        ("rs2", v((8, 8, 8, 128), F32)),
        ("g2t", v((2, 8, 8, 128), F32)),
        ("rg2", v((2, 8, 8, 8, 128), F32)),
        ("x2", v((18, 16, 128), F32)),
        ("y2", v((18, 16, 128), F32)),
        ("g2", v((16, 16, 128), F32)),
        ("s2", v((16, 16, 128), F32)),
        ("w2", v((16, 16, 128), F32)),
        ("dg2", v((16, 16, 128), F32)),
        ("pe2", v((8, 16, 128), F32)),
        ("tile", v((3, 4, 128), F32)),
        ("p1", v((3, 7, 4, 128), F32)),
        ("agb", v((3, ngx, 4, 128), F32)),
        ("dg3", v((ngx // 2, 8, 128), F32)),
        ("e3", v((ngx // 2, 8, 128), F32)),
        ("snd", pltpu.SemaphoreType.DMA((8, 8))),
        ("rcv", pltpu.SemaphoreType.DMA((8, 8))),
        ("ags", pltpu.SemaphoreType.DMA((3, 4))),
        ("loc", pltpu.SemaphoreType.DMA((2,))),
    )


EX_IN, EX_FACE, EX_S1, EX_S2, EX_B, EX_G = 0, 1, 2, 3, 4, 6


def kernel(ngx, ngy, names, pc_hbm, fc_hbm, sol_ref, res_ref, *scratch):
    m = dict(zip(names, scratch))
    gx = lax.axis_index("gx")
    gy = lax.axis_index("gy")
    half = ngx // 2
    nx0, ny0 = 16 * ngx, 16 * ngy

    def wrap_x(v):
        return lax.rem(v + ngx, ngx)

    def wrap_y(v):
        return lax.rem(v + ngy, ngy)

    copy_p = pltpu.make_async_copy(pc_hbm, m["pcv"], m["loc"].at[0])
    copy_f = pltpu.make_async_copy(fc_hbm, m["fcv"], m["loc"].at[1])
    copy_p.start()
    copy_f.start()

    barrier = pltpu.get_barrier_semaphore()
    peers = 0
    for o in range(1, ngy):
        pl.semaphore_signal(barrier, inc=1, device_id=(gx, wrap_y(gy + o)), device_id_type=MESH)
        peers += 1

    def greet(o, carry):
        pl.semaphore_signal(barrier, inc=1, device_id=(wrap_x(gx + o), gy), device_id_type=MESH)
        return carry

    lax.fori_loop(1, ngx, greet, 0)
    peers += ngx - 1
    for dx, dy in NEIGH:
        if dx != 0 and dy != 0:
            pl.semaphore_signal(
                barrier, inc=1, device_id=(wrap_x(gx + dx), wrap_y(gy + dy)), device_id_type=MESH
            )
            peers += 1

    for name in ("x0", "y0", "x1", "y1", "x2", "y2"):
        ref = m[name]
        last = ref.shape[0] - 1
        ref[0] = jnp.zeros(ref.shape[1:], F32)
        ref[last] = jnp.zeros(ref.shape[1:], F32)

    spans = {1: (8, 8, 0), 0: (0, 16, 8), -1: (0, 8, 24)}
    tiles = {1: (1, 1, 0), 0: (0, 2, 1), -1: (0, 1, 3)}

    def exists(dx, dy):
        x, y = gx + dx, gy + dy
        return (x >= 0) & (x < ngx) & (y >= 0) & (y < ngy)

    for n, (dx, dy) in enumerate(NEIGH):

        @pl.when(jnp.logical_not(exists(-dx, -dy)))
        def _():
            _, xn, xd = spans[dx]
            _, yn, yd = tiles[dy]
            m["ext"][xd : xd + xn, yd : yd + yn] = jnp.zeros((xn, yn, 16, 128), BF16)
            for name in ("rex", "rs1", "rs2"):
                m[name][n] = jnp.zeros(m[name].shape[1:], m[name].dtype)
            for name in ("rb", "rg2"):
                for c in range(2):
                    m[name][c, n] = jnp.zeros(m[name].shape[2:], F32)

    copy_f.wait()
    copy_p.wait()
    fcv, pcv = m["fcv"], m["pcv"]

    def own_rows(i):
        def counts(d, at, n):
            return fcv[d, pl.ds(at, n)].astype(F32) * 0.125

        f0, f1, f2 = counts(0, i, 4), counts(1, i, 4), counts(2, i, 4)
        before = jnp.where(i > 0, counts(0, jnp.maximum(i - 1, 0), 1), 0.0)
        low_x = jnp.concatenate([before, f0[:3]], axis=0)
        low_y = jnp.where(rows(f1.shape) == 0, 0.0, roll(f1, 1, 1))
        low_z = jnp.where(lanes(f2.shape) == 0, 0.0, roll(f2, 1, 2))
        src = (low_x - f0) + (low_y - f1) + (low_z - f2)
        scr = pcv[pl.ds(i, 4)].astype(F32) * 0.25
        m["scrown"][pl.ds(i, 4)] = scr
        for t in range(2):
            part = slice(8 * t, 8 * t + 8)
            m["ext"][pl.ds(i + 8, 4), t + 1] = jnp.concatenate([src[:, part], scr[:, part]], axis=1).astype(BF16)

    sweep(0, 16, 4, own_rows)

    tile_shape = (8, 128)
    sub = rows(tile_shape)
    lane = lanes(tile_shape)
    face_x = fcv[0, 15].astype(F32) * 0.125
    own_fx = [face_x[0:8], face_x[8:16]]
    own_fy = []
    for h in range(2):
        total = jnp.zeros(tile_shape, F32)
        for r in range(8):
            row = fcv[1, 8 * h + r, 15:16].astype(F32) * 0.125
            total = jnp.where(sub == r, row, total)
        own_fy.append(total)
    for t in range(2):
        m["exs"][t] = jnp.concatenate([own_fx[t], own_fy[t]], axis=0).astype(BF16)

    pl.semaphore_wait(barrier, peers)

    sent = []

    def exchange(kind, make):
        copies = []
        for n, (dx, dy) in enumerate(NEIGH):
            src, dst = make(n, dx, dy)
            copy = pltpu.make_async_remote_copy(
                src_ref=src,
                dst_ref=dst,
                send_sem=m["snd"].at[kind, n],
                recv_sem=m["rcv"].at[kind, n],
                device_id=(wrap_x(gx + dx), wrap_y(gy + dy)),
                device_id_type=MESH,
            )
            pl.when(exists(dx, dy))(copy.start)
            copies.append(copy)
        sent.append(copies)
        return copies

    def arrive(copies):
        for copy, (dx, dy) in zip(copies, NEIGH):
            pl.when(exists(-dx, -dy))(copy.wait_recv)

    def from_source(px, py):
        return NEIGH.index((-px, -py))

    def make_in(n, dx, dy):
        xs, xn, xd = spans[dx]
        ys, yn, yd = tiles[dy]
        src = m["ext"].at[pl.ds(xs + 8, xn), pl.ds(ys + 1, yn)]
        dst = m["ext"].at[pl.ds(xd, xn), pl.ds(yd, yn)]
        return src, dst

    copies_face = exchange(EX_FACE, lambda n, dx, dy: (m["exs"], m["rex"].at[n]))
    copies_in = exchange(EX_IN, make_in)

    own1 = []
    for i in range(8):
        total = jnp.zeros(tile_shape, F32)
        for q in range(2):
            for j in range(2):
                total = total + m["scrown"][2 * i + q, pl.ds(j, 8, stride=2), :]
        v = zpair(total, 1) * 0.125
        m["s1own"][i] = v
        own1.append(v)
    for k in range(4):
        m["s1p"][k] = jnp.concatenate([own1[2 * k], own1[2 * k + 1]], axis=0).astype(BF16)
    copies_s1 = exchange(EX_S1, lambda n, dx, dy: (m["s1p"], m["rs1"].at[n]))

    own3 = []
    for xi in range(2):
        pair = jnp.zeros((4, 128), F32)
        for q in range(2):
            quad = jnp.zeros((4, 128), F32)
            for h in range(2):
                for j in range(2):
                    quad = quad + m["s1own"][4 * xi + 2 * q + h, pl.ds(j, 4, stride=2), :]
            pair = pair + zpair(quad, 2) * 0.125
        pair = zpair(pair, 4) * 0.125
        own3 += [pair[0:1] + pair[1:2], pair[2:3] + pair[3:4]]
    m["tile"][2] = jnp.concatenate(own3, axis=0)

    def gather_one(c):
        for o in range(1, ngy):
            pltpu.make_async_remote_copy(
                src_ref=m["tile"].at[c],
                dst_ref=m["p1"].at[c, o - 1],
                send_sem=m["ags"].at[c, 0],
                recv_sem=m["ags"].at[c, 1],
                device_id=(gx, wrap_y(gy + o)),
                device_id_type=MESH,
            ).start()

    def wait_bytes(ref, sem):
        pltpu.make_async_copy(ref, ref, sem).wait()

    def gather_two(c):
        wait_bytes(m["p1"].at[c, pl.ds(0, ngy - 1)], m["ags"].at[c, 1])
        slot = lanes((4, 128)) & 7
        total = jnp.where(slot == gy, m["tile"][c], 0.0)
        for o in range(1, ngy):
            total = jnp.where(slot == wrap_y(gy - o), m["p1"][c, o - 1], total)
        m["agb"][c, gx] = total

        def send(o, carry):
            pltpu.make_async_remote_copy(
                src_ref=m["agb"].at[c, gx],
                dst_ref=m["agb"].at[c, gx],
                send_sem=m["ags"].at[c, 2],
                recv_sem=m["ags"].at[c, 3],
                device_id=(wrap_x(gx + o), gy),
                device_id_type=MESH,
            ).start()
            return carry

        lax.fori_loop(1, ngx, send, 0)

    def gather_done(c):
        wait_bytes(m["agb"].at[c, pl.ds(0, ngx - 1)], m["ags"].at[c, 3])
        return jnp.concatenate([m["agb"][c, 0:half], m["agb"][c, half:ngx]], axis=1)

    gather_one(2)

    arrive(copies_face)
    gate_x = jnp.where(gx > 0, 1.0, 0.0)
    gate_y = jnp.where(gy > 0, 1.0, 0.0)

    def face(px, py, t):
        return m["rex"][from_source(px, py), t].astype(F32)

    m["fy1"][0:8] = face(-1, -1, 1)[8:16] * gate_y
    m["fy1"][8:16] = face(0, -1, 0)[8:16] * gate_y
    m["fy1"][16:24] = face(0, -1, 1)[8:16] * gate_y
    m["fy1"][24:32] = face(1, -1, 0)[8:16] * gate_y
    m["fy2"][0:8] = face(-1, 0, 1)[8:16]
    m["fy2"][8:16] = own_fy[0]
    m["fy2"][16:24] = own_fy[1]
    m["fy2"][24:32] = face(1, 0, 0)[8:16]
    arrive(copies_in)

    def inside(shape, i, level, off):
        x = lax.broadcasted_iota(jnp.int32, shape, 0) + (i - off + gx * (16 >> level))
        y = rows(shape) + (gy * (16 >> level) - off)
        return (x >= 0) & (x < (nx0 >> level)) & (y >= 0) & (y < (ny0 >> level))

    def weight(dg, i, level, off):
        return jnp.where(inside(dg.shape, i, level, off), C1 / dg, 0.0)

    def unpack_in(i):
        n = 2
        for t in range(4):
            part = slice(8 * t, 8 * t + 8)
            pair = m["ext"][pl.ds(i, n), t].astype(F32)
            src = pair[:, 0:8]
            if t % 2 == 1:
                edge = m["fy1" if t == 1 else "fy2"]
                src = jnp.concatenate(
                    [(src[q] + jnp.where(sub == 0, edge[pl.ds(i + q, 1)], 0.0))[None] for q in range(n)], axis=0
                )
            dg = 6.0 + pair[:, 8:16]
            x = lax.broadcasted_iota(jnp.int32, dg.shape, 0) + (i - 8 + gx * 16)
            y = rows(dg.shape) + (gy * 16 - 8 + 8 * t)
            mask = (x >= 0) & (x < nx0) & (y >= 0) & (y < ny0)
            w = jnp.where(mask, C1 / dg, 0.0)
            m["g0"][pl.ds(i, n), part] = src
            m["dg0"][pl.ds(i, n), part] = dg
            m["w0"][pl.ds(i, n), part] = w
            m["x0"][pl.ds(i + 1, n), part] = src * w

    sweep(0, 32, 2, unpack_in)
    for t, (py, k) in enumerate(((-1, 1), (0, 0), (0, 1), (1, 0))):
        part = slice(8 * t, 8 * t + 8)
        upper = own_fx[k] if py == 0 else face(0, py, k)[0:8]
        for at, extra in ((8, face(-1, py, k)[0:8] * gate_x), (24, upper)):
            total = m["g0"][at, part] + extra
            m["g0"][at, part] = total
            m["x0"][at + 1, part] = total * m["w0"][at, part]

    lv0 = Level(m["x0"], m["y0"], m["g0"], m["w0"], m["dg0"], 0, 4)
    lv1 = Level(m["x1"], m["y1"], m["g1"], m["w1"], m["dg1"], 1, 4)
    lv2 = Level(m["x2"], m["y2"], m["g2"], m["w2"], m["dg2"], 2, 16)

    def make_weights(level, scr, step, count, off):
        def body(i):
            dg = 6.0 + scr[pl.ds(i, step)] * float(4**level.depth)
            level.dg[pl.ds(i, step)] = dg
            level.w[pl.ds(i, step)] = weight(dg, i, level.depth, off)

        sweep(0, count, step, body)

    odd = (lane & 1) == 1
    copies_b = [None, None]
    copies_g = [None, None]

    def send_b(c):
        def store(i, n, r):
            m["r0"][pl.ds(i - 8, n)] = r[:, 8:24]

        lv0.residual(8, 24, store)
        fine = []
        for i in range(8):
            total = jnp.zeros(tile_shape, F32)
            for q in range(2):
                for j in range(2):
                    total = total + m["r0"][2 * i + q, pl.ds(j, 8, stride=2), :]
            v = zpair(total, 1) * 0.5
            m["g1"][8 + i, 8:16] = v
            fine.append(v)
        for k in range(4):
            m["pk"][c, k] = jnp.where(odd, fine[2 * k + 1], fine[2 * k])

        def make(n, dx, dy):
            count = 4 if dx == 0 or (c == 0 and dy == 0) else 3
            part = pl.ds(4 - count if dx == 1 else 0, count)
            return m["pk"].at[c, part], m["rb"].at[c, n, part]

        copies_b[c] = exchange(EX_B + c, make)

    def take_b(c):
        arrive(copies_b[c])
        for n, (dx, dy) in enumerate(NEIGH):
            base = 8 - 8 * dx
            part = slice(8 - 8 * dy, 16 - 8 * dy)
            ks = range(4) if dx == 0 or (c == 0 and dy == 0) else (range(1, 4) if dx == 1 else range(3))
            for k in ks:
                v = m["rb"][c, n, k]
                m["g1"][base + 2 * k, part] = jnp.where(odd, roll(v, 1, 1), v)
                m["g1"][base + 2 * k + 1, part] = jnp.where(odd, v, roll(v, 127, 1))

    def setup_level1():
        arrive(copies_s1)
        for i in range(8):
            m["s1"][8 + i, 8:16] = m["s1own"][i]
        for n, (dx, dy) in enumerate(NEIGH):
            base = 8 - 8 * dx
            part = slice(8 - 8 * dy, 16 - 8 * dy)
            for k in range(4):
                v = m["rs1"][n, k].astype(F32)
                m["s1"][base + 2 * k, part] = v[0:8]
                m["s1"][base + 2 * k + 1, part] = v[8:16]
        make_weights(lv1, m["s1"], 4, 24, 8)
        for i in range(8):
            total = jnp.zeros(tile_shape, F32)
            for q in range(2):
                for j in range(2):
                    total = total + m["s1"][4 + 2 * i + q, pl.ds(4 + j, 8, stride=2), :]
            m["s2t"][i] = zpair(total, 2) * 0.125
        m["w2t"][...] = weight(6.0 + m["s2t"][...] * 16.0, 0, 2, 2)

    def exchange_tile(kind, src, dst):
        def make(n, dx, dy):
            part = {1: pl.ds(0, 4), 0: pl.ds(0, 8), -1: pl.ds(4, 4)}[dx]
            return src.at[part], dst.at[n, part]

        return exchange(kind, make)

    def assemble(own, got, out):
        for i in range(16):
            px = -1 if i < 4 else (0 if i < 12 else 1)
            r = i - 4 * px - 4
            for py, part in ((-1, slice(0, 8)), (1, slice(8, 16)), (0, slice(4, 12))):
                out[i, part] = own[r] if (px, py) == (0, 0) else got[from_source(px, py), r]

    def pre_level1(c):
        lv1.first_zero(0, 24)
        lv1.second_zero(0, 24)

        def store(i, n, r):
            m["r1"][pl.ds(i - 4, n)] = r

        lv1.residual(4, 20, store)
        small = []
        for i in range(8):
            total = jnp.zeros(tile_shape, F32)
            for q in range(2):
                for j in range(2):
                    total = total + m["r1"][2 * i + q, pl.ds(4 + j, 8, stride=2), :]
            small.append((zpair(total, 2) * 0.5)[None])
        g = jnp.concatenate(small, axis=0)
        m["g2t"][c] = g
        dg = 6.0 + m["s2t"][...] * 16.0
        w = m["w2t"][...]
        zero = jnp.zeros((1, 8, 128), F32)

        def around(v):
            up = jnp.concatenate([v[1:], zero], axis=0)
            dn = jnp.concatenate([zero, v[:-1]], axis=0)
            return g + side_sum(v, up, dn, 4)

        v = g * w
        v = K1 * v + K2 * (around(v) * w)
        r = around(v) - dg * v
        parts = []
        for xi in range(2):
            t = r[2 + 2 * xi] + r[3 + 2 * xi]
            t = zpair(t + roll(t, 7, 0), 4) * 0.5
            parts += [t[2:3], t[4:5]]
        m["tile"][c] = jnp.concatenate(parts, axis=0)

    def dot(a, b):
        t = jnp.sum(a * b, axis=0)
        t = jnp.sum(t, axis=0, keepdims=True)
        return jnp.sum(t, axis=1, keepdims=True)[None]

    full = (half, 8, 128)
    lane3 = lanes(full)
    sub3 = rows(full)
    slot3 = lane3 & 7
    even_y = (sub3 & 1) == 0
    even_x = (sub3 & 2) == 0
    low_y = even_y & (slot3 > 0)
    high_y = jnp.logical_not(even_y) & (slot3 < ngy - 1)

    def image3(f, dg):
        swap = jnp.where(even_y, roll(f, 7, 1), roll(f, 1, 1))
        total = swap + jnp.where(low_y, roll(swap, 1, 2), jnp.where(high_y, roll(swap, 127, 2), 0.0))
        left = roll(f, 6, 1)
        right = roll(f, 2, 1)
        after = jnp.where(sub < 4, left[0], 0.0)[None]
        ahead = jnp.where(sub >= 4, right[half - 1], 0.0)[None]
        nxt = jnp.concatenate([right[1:], after], axis=0)
        prv = jnp.concatenate([ahead, left[:-1]], axis=0)
        total = total + jnp.where(even_x, left + prv, right + nxt)
        total = total + jnp.where(lane3 < 8, 0.0, roll(f, 8, 2))
        total = total + jnp.where(lane3 >= 120, 0.0, roll(f, 120, 2))
        q = dg * f - total
        return q if ngy == 8 else jnp.where(slot3 < ngy, q, 0.0)

    def coarse(r):
        dg = m["dg3"][...]
        x = p = q = rr_old = curve = None
        for it in range(COARSE_ITERS):
            image = image3(r, dg)
            rr = dot(r, r)
            rar = dot(r, image)
            if it == 0:
                p, q, curve = r, image, rar
            else:
                beta = rr / rr_old
                curve = rar - beta * beta * curve
                p = r + beta * p
                q = image + beta * q
            alpha = rr / curve
            x = alpha * p if it == 0 else x + alpha * p
            if it + 1 < COARSE_ITERS:
                r = r - alpha * q
            rr_old = rr
        m["e3"][...] = x

    step_y = (sub + 1) >> 1
    pick = (lane & 7) == step_y

    def post_level2():
        for k in range(8):
            a, xi = (k - 3) >> 1, (k - 3) & 1
            at = wrap_x(gx + a)
            b = at // half
            v = at - b * half
            low = m["e3"][v, pl.ds(4 * b + 2 * xi, 1)]
            high = m["e3"][v, pl.ds(4 * b + 2 * xi + 1, 1)]
            t = jnp.where((sub & 1) == 1, low, high)
            t = roll(t, lax.rem(130 - gy, 128), 1)
            t = jnp.where(pick, t, 0.0)
            for width in (4, 2, 1):
                t = jnp.where((step_y & width) != 0, roll(t, 128 - width, 1), t)
            for width in (1, 2, 4):
                t = t + roll(t, width, 1)
            m["pe2"][k, pl.ds(0, 8, stride=2), :] = t
            m["pe2"][k, pl.ds(1, 8, stride=2), :] = t
        for i in range(16):
            m["y2"][i + 1] = m["y2"][i + 1] + jnp.where(m["w2"][i] != 0.0, m["pe2"][i // 2], 0.0)
        lv2.pass_one(0, 16)
        lv2.pass_two(0, 16)

    def post_level1(c):
        lo, hi = ((2, 22), (4, 20))[c]
        for i in range(lo, hi):
            e = m["y2"][i // 2 + 3, 2:14]
            for j in range(2):
                at = pl.ds(j, 12, stride=2)
                m["y1"][i + 1, at, :] = m["y1"][i + 1, at, :] + e
        lv1.pass_one(lo, hi)
        if c == 0:
            lv1.pass_two(4, 20)
        else:
            lv1.pass_two(6, 18)

    def post_level0(c):
        lo, hi = ((0, 32), (4, 28))[c]

        def add(k):
            for h in range(2):
                e = m["y1"][k + h + 5, 4:20]
                for q in range(2):
                    for j in range(2):
                        at = pl.ds(j, 16, stride=2)
                        i = 2 * (k + h) + q + 1
                        m["y0"][i, at, :] = m["y0"][i, at, :] + e

        sweep(lo // 2, hi // 2, 2, add)
        lv0.pass_one(lo, hi)
        if c == 0:
            lv0.pass_two(2, 30)
        else:
            lv0.pass_two(lo, hi)

    for c in range(2):
        if c == 0:
            lv0.second_zero(0, 32)
        else:
            lv0.pass_one(4, 28)
            lv0.pass_two(4, 28)
        send_b(c)
        if c == 0:
            gather_two(2)
            setup_level1()
            copies_s2 = exchange_tile(EX_S2, m["s2t"], m["rs2"])
        take_b(c)
        pre_level1(c)
        gather_one(c)
        copies_g[c] = exchange_tile(EX_G + c, m["g2t"].at[c], m["rg2"].at[c])
        if c == 0:
            arrive(copies_s2)
            assemble(m["s2t"], m["rs2"], m["s2"])
            make_weights(lv2, m["s2"], 8, 16, 6)
        gather_two(c)
        arrive(copies_g[c])
        assemble(m["g2t"].at[c], m["rg2"].at[c], m["g2"])
        lv2.first_zero(0, 16)
        lv2.second_zero(0, 16)
        if c == 0:
            m["dg3"][...] = 6.0 + gather_done(2) * 64.0
        coarse(gather_done(c))
        post_level2()
        post_level1(c)
        post_level0(c)

    def store(i, n, r):
        res_ref[pl.ds(i - 8, n)] = r[:, 8:24]
        sol_ref[pl.ds(i - 8, n)] = m["y0"][pl.ds(i + 1, n), 8:24]

    lv0.residual(8, 24, store)

    for copies in sent:
        for copy, (dx, dy) in zip(copies, NEIGH):
            pl.when(exists(dx, dy))(copy.wait_send)
    for c in range(3):
        wait_bytes(m["p1"].at[c, pl.ds(0, ngy - 1)], m["ags"].at[c, 0])
        wait_bytes(m["agb"].at[c, pl.ds(0, ngx - 1)], m["ags"].at[c, 2])


def solution(mesh):
    ngx, ngy = mesh.shape["gx"], mesh.shape["gy"]
    items = scratch_list(ngx)
    names = tuple(name for name, _ in items)

    def per_device(point_counts, face_counts):
        shape = jax.ShapeDtypeStruct(point_counts.shape, F32)
        return pl.pallas_call(
            functools.partial(kernel, ngx, ngy, names),
            out_shape=(shape, shape),
            in_specs=[pl.BlockSpec(memory_space=pltpu.HBM)] * 2,
            out_specs=(pl.BlockSpec(memory_space=pltpu.VMEM),) * 2,
            scratch_shapes=[spec for _, spec in items],
            compiler_params=pltpu.CompilerParams(
                collective_id=0, has_side_effects=True, vmem_limit_bytes=48 * 1024 * 1024
            ),
            name="poisson",
        )(point_counts, face_counts)

    return jax.shard_map(
        per_device,
        mesh=mesh,
        in_specs=(P("gx", "gy", None), P(None, "gx", "gy", None)),
        out_specs=(P("gx", "gy", None), P("gx", "gy", None)),
        check_vma=False,
    )
```

time: 72.2 us -> 64.6 us (0.89)
  Pallas kernels: 68.3 us -> 60.6 us
    pallas_call x1, Pallas kernels: 68.3 us -> 60.6 us  [per_device(): pl.pallas_call(functools.partial(kernel, ngx, ngy, names), out_shape=(sha...]
where the time goes in v2:
time: 64.6 us; the launch traced here: 64.5 us
  Pallas kernels  60.6 us (94%)
  local copies, waits for them, and re-layouts  3.21 us (5%)
  between operations  0.65 us (1%)
    pallas_call x1, Pallas kernels, per_device(): pl.pallas_call(functools.partial(kernel, ngx, ngy, names), out_shape=(sha...  60.6 us
    unnamed x6, local copies, waits for them, and re-layouts  3.21 us

profile of v2, /device:TPU:1, one launch (start us, length us, event | category | flops | bytes accessed | tf_op | source)
XLA Modules:
  0.0 64.5 jit_solution(17042946796529802820)
XLA Ops:
  0.6 0.0 copy-start
  0.6 1.0 %copy-done = s32[3,16,16,128]{3,2,1,0:T(8,128)S(1)} copy-done((s32[3,16,16,128]{3,2,1,0:T(8,128)S(1)}, s32[3,16,16,128]{3,2,1,0:T(8,128)}, u32[]{:S(2)}) %copy-start) | copy-done | bytes 393240
  1.6 0.0 copy-start.1
  1.6 0.9 %copy-done.1 = s32[16,16,128]{2,1,0:T(8,128)S(1)} copy-done((s32[16,16,128]{2,1,0:T(8,128)S(1)}, s32[16,16,128]{2,1,0:T(8,128)}, u32[]{:S(2)}) %copy-start.1) | copy-done | bytes 131096
  2.5 60.6 %poisson.1 = (f32[16,16,128]{2,1,0:T(8,128)S(1)}, f32[16,16,128]{2,1,0:T(8,128)S(1)}) custom-call(s32[16,16,128]{2,1,0:T(8,128)S(1)} %copy-done.1, s32[3,16,16,128]{3,2,1,0:T(8,128)S(1)} %copy-done), custom_call_target="tpu_custom_call" | custom-call | tf_op jit(solution)/shard_map/poisson/pallas_call | solution.py:721
  63.2 0.7 %copy.6 = f32[16,16,128]{2,1,0:T(8,128)} copy(f32[16,16,128]{2,1,0:T(8,128)S(1)} %get-tuple-element.4) | data formatting | bytes 262144
  63.8 0.7 %copy.7 = f32[16,16,128]{2,1,0:T(8,128)} copy(f32[16,16,128]{2,1,0:T(8,128)S(1)} %get-tuple-element.5) | data formatting | bytes 262144
Async XLA Ops:
  0.6 1.0 %copy-start = (s32[3,16,16,128]{3,2,1,0:T(8,128)S(1)}, s32[3,16,16,128]{3,2,1,0:T(8,128)}, u32[]{:S(2)}) copy-start(s32[3,16,16,128]{3,2,1,0:T(8,128)} %fc_hbm.1) | copy-start | bytes 1179652
  1.6 0.9 %copy-start.1 = (s32[16,16,128]{2,1,0:T(8,128)S(1)}, s32[16,16,128]{2,1,0:T(8,128)}, u32[]{:S(2)}) copy-start(s32[16,16,128]{2,1,0:T(8,128)} %pc_hbm.1) | copy-start | bytes 393220

commit v3 on v2

--- a/solution.py
+++ b/solution.py
@@ -61,60 +61,55 @@
         body(lo + k * step)
         return carry
 
-    lax.fori_loop(0, (hi - lo) // step, one, 0)
+    lax.fori_loop(0, (hi - lo) // step, one, 0, unroll=True)
 
 
 class Level:
-    def __init__(self, x, y, g, w, dg, depth, step):
+    def __init__(self, x, y, g, w, dg, depth):
         self.x, self.y, self.g, self.w, self.dg = x, y, g, w, dg
         self.depth = depth
         self.shift = 2**depth
-        self.step = step
+        self.count = g.shape[1]
+        self.mid = slice(8, 8 + self.count)
 
     def around(self, src, i, n):
-        c = src[pl.ds(i + 1, n)]
-        total = side_sum(c, src[pl.ds(i + 2, n)], src[pl.ds(i, n)], self.shift)
-        return c, total + self.g[pl.ds(i, n)]
-
-    def first_zero(self, lo, hi):
-        n = self.step
-
+        c = src[pl.ds(i + 1, n), self.mid]
+        lane = lanes(c.shape)
+        total = src[pl.ds(i + 2, n), self.mid] + src[pl.ds(i, n), self.mid]
+        total = total + (src[pl.ds(i + 1, n), 7 : 7 + self.count] + src[pl.ds(i + 1, n), 9 : 9 + self.count])
+        low = jnp.where(lane < self.shift, 0.0, roll(c, self.shift, 2))
+        high = jnp.where(lane >= 128 - self.shift, 0.0, roll(c, 128 - self.shift, 2))
+        return c, (total + self.g[pl.ds(i, n)]) + (low + high)
+
+    def first_zero(self, lo, hi, n):
         def body(i):
-            self.x[pl.ds(i + 1, n)] = self.g[pl.ds(i, n)] * self.w[pl.ds(i, n)]
+            self.x[pl.ds(i + 1, n), self.mid] = self.g[pl.ds(i, n)] * self.w[pl.ds(i, n)]
 
         sweep(lo, hi, n, body)
 
-    def second_zero(self, lo, hi):
-        n = self.step
-
+    def second_zero(self, lo, hi, n):
         def body(i):
             c, t = self.around(self.x, i, n)
-            self.y[pl.ds(i + 1, n)] = K1 * c + K2 * (t * self.w[pl.ds(i, n)])
+            self.y[pl.ds(i + 1, n), self.mid] = K1 * c + K2 * (t * self.w[pl.ds(i, n)])
 
         sweep(lo, hi, n, body)
 
-    def pass_one(self, lo, hi):
-        n = self.step
-
+    def pass_one(self, lo, hi, n):
         def body(i):
             c, t = self.around(self.y, i, n)
-            self.x[pl.ds(i + 1, n)] = K0 * c + t * self.w[pl.ds(i, n)]
+            self.x[pl.ds(i + 1, n), self.mid] = K0 * c + t * self.w[pl.ds(i, n)]
 
         sweep(lo, hi, n, body)
 
-    def pass_two(self, lo, hi):
-        n = self.step
-
+    def pass_two(self, lo, hi, n):
         def body(i):
             c, t = self.around(self.x, i, n)
-            old = self.y[pl.ds(i + 1, n)]
-            self.y[pl.ds(i + 1, n)] = (K1 * c - CA * old) + K2 * (t * self.w[pl.ds(i, n)])
+            old = self.y[pl.ds(i + 1, n), self.mid]
+            self.y[pl.ds(i + 1, n), self.mid] = (K1 * c - CA * old) + K2 * (t * self.w[pl.ds(i, n)])
 
         sweep(lo, hi, n, body)
 
-    def residual(self, lo, hi, store):
-        n = self.step
-
+    def residual(self, lo, hi, n, store):
         def body(i):
             c, t = self.around(self.y, i, n)
             store(i, n, t - self.dg[pl.ds(i, n)] * c)
@@ -136,16 +131,16 @@
         ("s1own", v((8, 8, 128), F32)),
         ("fy1", v((32, 128), F32)),
         ("fy2", v((32, 128), F32)),
-        ("x0", v((34, 32, 128), F32)),
-        ("y0", v((34, 32, 128), F32)),
+        ("x0", v((34, 48, 128), F32)),
+        ("y0", v((34, 48, 128), F32)),
         ("g0", v((32, 32, 128), F32)),
         ("w0", v((32, 32, 128), F32)),
         ("dg0", v((32, 32, 128), F32)),
         ("r0", v((16, 16, 128), F32)),
         ("pk", v((2, 4, 8, 128), F32)),
         ("rb", v((2, 8, 4, 8, 128), F32)),
-        ("x1", v((26, 24, 128), F32)),
-        ("y1", v((26, 24, 128), F32)),
+        ("x1", v((26, 40, 128), F32)),
+        ("y1", v((26, 40, 128), F32)),
         ("g1", v((24, 24, 128), F32)),
         ("s1", v((24, 24, 128), F32)),
         ("w1", v((24, 24, 128), F32)),
@@ -156,8 +151,8 @@
         ("rs2", v((8, 8, 8, 128), F32)),
         ("g2t", v((2, 8, 8, 128), F32)),
         ("rg2", v((2, 8, 8, 8, 128), F32)),
-        ("x2", v((18, 16, 128), F32)),
-        ("y2", v((18, 16, 128), F32)),
+        ("x2", v((18, 32, 128), F32)),
+        ("y2", v((18, 32, 128), F32)),
         ("g2", v((16, 16, 128), F32)),
         ("s2", v((16, 16, 128), F32)),
         ("w2", v((16, 16, 128), F32)),
@@ -214,12 +209,6 @@
                 barrier, inc=1, device_id=(wrap_x(gx + dx), wrap_y(gy + dy)), device_id_type=MESH
             )
             peers += 1
-
-    for name in ("x0", "y0", "x1", "y1", "x2", "y2"):
-        ref = m[name]
-        last = ref.shape[0] - 1
-        ref[0] = jnp.zeros(ref.shape[1:], F32)
-        ref[last] = jnp.zeros(ref.shape[1:], F32)
 
     spans = {1: (8, 8, 0), 0: (0, 16, 8), -1: (0, 8, 24)}
     tiles = {1: (1, 1, 0), 0: (0, 2, 1), -1: (0, 1, 3)}
@@ -316,6 +305,14 @@
     copies_face = exchange(EX_FACE, lambda n, dx, dy: (m["exs"], m["rex"].at[n]))
     copies_in = exchange(EX_IN, make_in)
 
+    for name in ("x0", "y0", "x1", "y1", "x2", "y2"):
+        ref = m[name]
+        count, width = ref.shape[:2]
+        ref[0] = jnp.zeros((width, 128), F32)
+        ref[count - 1] = jnp.zeros((width, 128), F32)
+        ref[1 : count - 1, 0:8] = jnp.zeros((count - 2, 8, 128), F32)
+        ref[1 : count - 1, width - 8 : width] = jnp.zeros((count - 2, 8, 128), F32)
+
     own1 = []
     for i in range(8):
         total = jnp.zeros(tile_shape, F32)
@@ -364,7 +361,7 @@
             total = jnp.where(slot == wrap_y(gy - o), m["p1"][c, o - 1], total)
         m["agb"][c, gx] = total
 
-        def send(o, carry):
+        for o in sorted(range(1, ngx), key=lambda o: -(min(o % 8, 8 - o % 8) + min(o // 8, 4 - o // 8))):
             pltpu.make_async_remote_copy(
                 src_ref=m["agb"].at[c, gx],
                 dst_ref=m["agb"].at[c, gx],
@@ -373,9 +370,6 @@
                 device_id=(wrap_x(gx + o), gy),
                 device_id_type=MESH,
             ).start()
-            return carry
-
-        lax.fori_loop(1, ngx, send, 0)
 
     def gather_done(c):
         wait_bytes(m["agb"].at[c, pl.ds(0, ngx - 1)], m["ags"].at[c, 3])
@@ -409,7 +403,7 @@
         return jnp.where(inside(dg.shape, i, level, off), C1 / dg, 0.0)
 
     def unpack_in(i):
-        n = 2
+        n = 4
         for t in range(4):
             part = slice(8 * t, 8 * t + 8)
             pair = m["ext"][pl.ds(i, n), t].astype(F32)
@@ -427,20 +421,20 @@
             m["g0"][pl.ds(i, n), part] = src
             m["dg0"][pl.ds(i, n), part] = dg
             m["w0"][pl.ds(i, n), part] = w
-            m["x0"][pl.ds(i + 1, n), part] = src * w
-
-    sweep(0, 32, 2, unpack_in)
+            m["x0"][pl.ds(i + 1, n), 8 * t + 8 : 8 * t + 16] = src * w
+
+    sweep(0, 32, 4, unpack_in)
     for t, (py, k) in enumerate(((-1, 1), (0, 0), (0, 1), (1, 0))):
         part = slice(8 * t, 8 * t + 8)
         upper = own_fx[k] if py == 0 else face(0, py, k)[0:8]
         for at, extra in ((8, face(-1, py, k)[0:8] * gate_x), (24, upper)):
             total = m["g0"][at, part] + extra
             m["g0"][at, part] = total
-            m["x0"][at + 1, part] = total * m["w0"][at, part]
-
-    lv0 = Level(m["x0"], m["y0"], m["g0"], m["w0"], m["dg0"], 0, 4)
-    lv1 = Level(m["x1"], m["y1"], m["g1"], m["w1"], m["dg1"], 1, 4)
-    lv2 = Level(m["x2"], m["y2"], m["g2"], m["w2"], m["dg2"], 2, 16)
+            m["x0"][at + 1, 8 * t + 8 : 8 * t + 16] = total * m["w0"][at, part]
+
+    lv0 = Level(m["x0"], m["y0"], m["g0"], m["w0"], m["dg0"], 0)
+    lv1 = Level(m["x1"], m["y1"], m["g1"], m["w1"], m["dg1"], 1)
+    lv2 = Level(m["x2"], m["y2"], m["g2"], m["w2"], m["dg2"], 2)
 
     def make_weights(level, scr, step, count, off):
         def body(i):
@@ -458,7 +452,7 @@
         def store(i, n, r):
             m["r0"][pl.ds(i - 8, n)] = r[:, 8:24]
 
-        lv0.residual(8, 24, store)
+        lv0.residual(8, 24, 8, store)
         fine = []
         for i in range(8):
             total = jnp.zeros(tile_shape, F32)
@@ -500,7 +494,7 @@
                 v = m["rs1"][n, k].astype(F32)
                 m["s1"][base + 2 * k, part] = v[0:8]
                 m["s1"][base + 2 * k + 1, part] = v[8:16]
-        make_weights(lv1, m["s1"], 4, 24, 8)
+        make_weights(lv1, m["s1"], 8, 24, 8)
         for i in range(8):
             total = jnp.zeros(tile_shape, F32)
             for q in range(2):
@@ -524,13 +518,13 @@
                 out[i, part] = own[r] if (px, py) == (0, 0) else got[from_source(px, py), r]
 
     def pre_level1(c):
-        lv1.first_zero(0, 24)
-        lv1.second_zero(0, 24)
+        lv1.first_zero(0, 24, 8)
+        lv1.second_zero(0, 24, 8)
 
         def store(i, n, r):
             m["r1"][pl.ds(i - 4, n)] = r
 
-        lv1.residual(4, 20, store)
+        lv1.residual(4, 20, 8, store)
         small = []
         for i in range(8):
             total = jnp.zeros(tile_shape, F32)
@@ -560,8 +554,11 @@
         m["tile"][c] = jnp.concatenate(parts, axis=0)
 
     def dot(a, b):
-        t = jnp.sum(a * b, axis=0)
-        t = jnp.sum(t, axis=0, keepdims=True)
+        t = a * b
+        while t.shape[0] > 1:
+            h = t.shape[0] // 2
+            t = t[:h] + t[h:]
+        t = jnp.sum(t[0], axis=0, keepdims=True)
         return jnp.sum(t, axis=1, keepdims=True)[None]
 
     full = (half, 8, 128)
@@ -630,48 +627,50 @@
             m["pe2"][k, pl.ds(0, 8, stride=2), :] = t
             m["pe2"][k, pl.ds(1, 8, stride=2), :] = t
         for i in range(16):
-            m["y2"][i + 1] = m["y2"][i + 1] + jnp.where(m["w2"][i] != 0.0, m["pe2"][i // 2], 0.0)
-        lv2.pass_one(0, 16)
-        lv2.pass_two(0, 16)
+            m["y2"][i + 1, 8:24] = m["y2"][i + 1, 8:24] + jnp.where(m["w2"][i] != 0.0, m["pe2"][i // 2], 0.0)
+        lv2.pass_one(1, 15, 14)
+        lv2.pass_two(2, 14, 12)
 
     def post_level1(c):
         lo, hi = ((2, 22), (4, 20))[c]
         for i in range(lo, hi):
-            e = m["y2"][i // 2 + 3, 2:14]
+            e = m["y2"][i // 2 + 3, 10:22]
             for j in range(2):
-                at = pl.ds(j, 12, stride=2)
+                at = pl.ds(8 + j, 12, stride=2)
                 m["y1"][i + 1, at, :] = m["y1"][i + 1, at, :] + e
-        lv1.pass_one(lo, hi)
         if c == 0:
-            lv1.pass_two(4, 20)
+            lv1.pass_one(3, 21, 9)
+            lv1.pass_two(4, 20, 8)
         else:
-            lv1.pass_two(6, 18)
+            lv1.pass_one(5, 19, 7)
+            lv1.pass_two(6, 18, 6)
 
     def post_level0(c):
         lo, hi = ((0, 32), (4, 28))[c]
 
         def add(k):
             for h in range(2):
-                e = m["y1"][k + h + 5, 4:20]
+                e = m["y1"][k + h + 5, 12:28]
                 for q in range(2):
                     for j in range(2):
-                        at = pl.ds(j, 16, stride=2)
+                        at = pl.ds(8 + j, 16, stride=2)
                         i = 2 * (k + h) + q + 1
                         m["y0"][i, at, :] = m["y0"][i, at, :] + e
 
         sweep(lo // 2, hi // 2, 2, add)
-        lv0.pass_one(lo, hi)
         if c == 0:
-            lv0.pass_two(2, 30)
+            lv0.pass_one(2, 30, 7)
+            lv0.pass_two(2, 30, 7)
         else:
-            lv0.pass_two(lo, hi)
+            lv0.pass_one(6, 26, 5)
+            lv0.pass_two(7, 25, 6)
 
     for c in range(2):
         if c == 0:
-            lv0.second_zero(0, 32)
+            lv0.second_zero(0, 32, 8)
         else:
-            lv0.pass_one(4, 28)
-            lv0.pass_two(4, 28)
+            lv0.pass_one(4, 28, 8)
+            lv0.pass_two(4, 28, 8)
         send_b(c)
         if c == 0:
             gather_two(2)
@@ -688,10 +687,17 @@
         gather_two(c)
         arrive(copies_g[c])
         assemble(m["g2t"].at[c], m["rg2"].at[c], m["g2"])
-        lv2.first_zero(0, 16)
-        lv2.second_zero(0, 16)
+        lv2.first_zero(0, 16, 16)
+        lv2.second_zero(1, 15, 14)
         if c == 0:
             m["dg3"][...] = 6.0 + gather_done(2) * 64.0
+        if c == 1:
+            for copies in sent:
+                for copy, (dx, dy) in zip(copies, NEIGH):
+                    pl.when(exists(dx, dy))(copy.wait_send)
+            for k in range(3):
+                wait_bytes(m["p1"].at[k, pl.ds(0, ngy - 1)], m["ags"].at[k, 0])
+                wait_bytes(m["agb"].at[k, pl.ds(0, ngx - 1)], m["ags"].at[k, 2])
         coarse(gather_done(c))
         post_level2()
         post_level1(c)
@@ -699,16 +705,9 @@
 
     def store(i, n, r):
         res_ref[pl.ds(i - 8, n)] = r[:, 8:24]
-        sol_ref[pl.ds(i - 8, n)] = m["y0"][pl.ds(i + 1, n), 8:24]
-
-    lv0.residual(8, 24, store)
-
-    for copies in sent:
-        for copy, (dx, dy) in zip(copies, NEIGH):
-            pl.when(exists(dx, dy))(copy.wait_send)
-    for c in range(3):
-        wait_bytes(m["p1"].at[c, pl.ds(0, ngy - 1)], m["ags"].at[c, 0])
-        wait_bytes(m["agb"].at[c, pl.ds(0, ngx - 1)], m["ags"].at[c, 2])
+        sol_ref[pl.ds(i - 8, n)] = m["y0"][pl.ds(i + 1, n), 16:32]
+
+    lv0.residual(8, 24, 8, store)
 
 
 def solution(mesh):
@@ -725,7 +724,7 @@
             out_specs=(pl.BlockSpec(memory_space=pltpu.VMEM),) * 2,
             scratch_shapes=[spec for _, spec in items],
             compiler_params=pltpu.CompilerParams(
-                collective_id=0, has_side_effects=True, vmem_limit_bytes=48 * 1024 * 1024
+                collective_id=0, has_side_effects=True, vmem_limit_bytes=54880 * 1024
             ),
             name="poisson",
         )(point_counts, face_counts)

time: 64.6 us -> 54.8 us (0.85)
  Pallas kernels: 60.6 us -> 52.8 us
  local copies, waits for them, and re-layouts: 3.21 us -> 1.31 us
    pallas_call x1, Pallas kernels: 60.6 us -> 52.8 us  [per_device(): pl.pallas_call(functools.partial(kernel, ngx, ngy, names), out_shape=(sha...]
    unnamed x6 -> x2, local copies, waits for them, and re-layouts: 3.21 us -> 1.31 us
where the time goes in v3:
time: 54.8 us; the launch traced here: 54.7 us
  Pallas kernels  52.8 us (96%)
  local copies, waits for them, and re-layouts  1.31 us (2%)
  between operations  0.64 us (1%)
    pallas_call x1, Pallas kernels, per_device(): pl.pallas_call(functools.partial(kernel, ngx, ngy, names), out_shape=(sha...  52.8 us
    unnamed x2, local copies, waits for them, and re-layouts  1.31 us

profile of v3, /device:TPU:1, one launch (start us, length us, event | category | flops | bytes accessed | tf_op | source)
XLA Modules:
  0.0 54.7 jit_solution(1555702398782653283)
XLA Ops:
  0.6 52.8 %poisson.1 = (f32[16,16,128]{2,1,0:T(8,128)S(1)}, f32[16,16,128]{2,1,0:T(8,128)S(1)}) custom-call(s32[16,16,128]{2,1,0:T(8,128)} %pc_hbm.1, s32[3,16,16,128]{3,2,1,0:T(8,128)} %fc_hbm.1), custom_call_target="tpu_custom_call" | custom-call | tf_op jit(solution)/shard_map/poisson/pallas_call | solution.py:720
  53.4 0.7 %copy.6 = f32[16,16,128]{2,1,0:T(8,128)} copy(f32[16,16,128]{2,1,0:T(8,128)S(1)} %get-tuple-element.4) | data formatting | bytes 262144
  54.1 0.7 %copy.7 = f32[16,16,128]{2,1,0:T(8,128)} copy(f32[16,16,128]{2,1,0:T(8,128)S(1)} %get-tuple-element.5) | data formatting | bytes 262144

commit v4 on v3

--- a/solution.py
+++ b/solution.py
@@ -62,6 +62,10 @@
         return carry
 
     lax.fori_loop(0, (hi - lo) // step, one, 0, unroll=True)
+
+
+def far_first(ngx):
+    return sorted(range(1, ngx), key=lambda o: -(min(o % 8, 8 - o % 8) + min(o // 8, 4 - o // 8)))
 
 
 class Level:
@@ -192,23 +196,13 @@
     copy_f.start()
 
     barrier = pltpu.get_barrier_semaphore()
-    peers = 0
-    for o in range(1, ngy):
-        pl.semaphore_signal(barrier, inc=1, device_id=(gx, wrap_y(gy + o)), device_id_type=MESH)
-        peers += 1
-
-    def greet(o, carry):
-        pl.semaphore_signal(barrier, inc=1, device_id=(wrap_x(gx + o), gy), device_id_type=MESH)
-        return carry
-
-    lax.fori_loop(1, ngx, greet, 0)
-    peers += ngx - 1
-    for dx, dy in NEIGH:
-        if dx != 0 and dy != 0:
-            pl.semaphore_signal(
-                barrier, inc=1, device_id=(wrap_x(gx + dx), wrap_y(gy + dy)), device_id_type=MESH
-            )
-            peers += 1
+    met = [(o, 0) for o in far_first(ngx)]
+    met += [(dx, dy) for dx, dy in NEIGH if dx != 0 and dy != 0]
+    met += [(0, o) for o in range(1, ngy)]
+    for dx, dy in met:
+        pl.semaphore_signal(
+            barrier, inc=1, device_id=(wrap_x(gx + dx), wrap_y(gy + dy)), device_id_type=MESH
+        )
 
     spans = {1: (8, 8, 0), 0: (0, 16, 8), -1: (0, 8, 24)}
     tiles = {1: (1, 1, 0), 0: (0, 2, 1), -1: (0, 1, 3)}
@@ -216,19 +210,6 @@
     def exists(dx, dy):
         x, y = gx + dx, gy + dy
         return (x >= 0) & (x < ngx) & (y >= 0) & (y < ngy)
-
-    for n, (dx, dy) in enumerate(NEIGH):
-
-        @pl.when(jnp.logical_not(exists(-dx, -dy)))
-        def _():
-            _, xn, xd = spans[dx]
-            _, yn, yd = tiles[dy]
-            m["ext"][xd : xd + xn, yd : yd + yn] = jnp.zeros((xn, yn, 16, 128), BF16)
-            for name in ("rex", "rs1", "rs2"):
-                m[name][n] = jnp.zeros(m[name].shape[1:], m[name].dtype)
-            for name in ("rb", "rg2"):
-                for c in range(2):
-                    m[name][c, n] = jnp.zeros(m[name].shape[2:], F32)
 
     copy_f.wait()
     copy_p.wait()
@@ -267,7 +248,7 @@
     for t in range(2):
         m["exs"][t] = jnp.concatenate([own_fx[t], own_fy[t]], axis=0).astype(BF16)
 
-    pl.semaphore_wait(barrier, peers)
+    pl.semaphore_wait(barrier, len(met))
 
     sent = []
 
@@ -302,8 +283,26 @@
         dst = m["ext"].at[pl.ds(xd, xn), pl.ds(yd, yn)]
         return src, dst
 
-    copies_face = exchange(EX_FACE, lambda n, dx, dy: (m["exs"], m["rex"].at[n]))
+    def make_face(n, dx, dy):
+        first, count = (0, 2) if (dx, dy) in ((1, 0), (0, 1)) else ((1, 1) if (dx, dy) == (1, 1) else (0, 1))
+        part = pl.ds(first, count)
+        return m["exs"].at[part], m["rex"].at[n, part]
+
+    copies_face = exchange(EX_FACE, make_face)
     copies_in = exchange(EX_IN, make_in)
+
+    for n, (dx, dy) in enumerate(NEIGH):
+
+        @pl.when(jnp.logical_not(exists(-dx, -dy)))
+        def _():
+            _, xn, xd = spans[dx]
+            _, yn, yd = tiles[dy]
+            m["ext"][xd : xd + xn, yd : yd + yn] = jnp.zeros((xn, yn, 16, 128), BF16)
+            for name in ("rex", "rs1", "rs2"):
+                m[name][n] = jnp.zeros(m[name].shape[1:], m[name].dtype)
+            for name in ("rb", "rg2"):
+                for c in range(2):
+                    m[name][c, n] = jnp.zeros(m[name].shape[2:], F32)
 
     for name in ("x0", "y0", "x1", "y1", "x2", "y2"):
         ref = m[name]
@@ -361,7 +360,7 @@
             total = jnp.where(slot == wrap_y(gy - o), m["p1"][c, o - 1], total)
         m["agb"][c, gx] = total
 
-        for o in sorted(range(1, ngx), key=lambda o: -(min(o % 8, 8 - o % 8) + min(o // 8, 4 - o // 8))):
+        for o in far_first(ngx):
             pltpu.make_async_remote_copy(
                 src_ref=m["agb"].at[c, gx],
                 dst_ref=m["agb"].at[c, gx],
@@ -606,8 +605,7 @@
             rr_old = rr
         m["e3"][...] = x
 
-    step_y = (sub + 1) >> 1
-    pick = (lane & 7) == step_y
+    pick = (lane - (lane & 7)) + jnp.clip(gy - 2 + ((sub + 1) >> 1), 0, ngy - 1)
 
     def post_level2():
         for k in range(8):
@@ -618,12 +616,7 @@
             low = m["e3"][v, pl.ds(4 * b + 2 * xi, 1)]
             high = m["e3"][v, pl.ds(4 * b + 2 * xi + 1, 1)]
             t = jnp.where((sub & 1) == 1, low, high)
-            t = roll(t, lax.rem(130 - gy, 128), 1)
-            t = jnp.where(pick, t, 0.0)
-            for width in (4, 2, 1):
-                t = jnp.where((step_y & width) != 0, roll(t, 128 - width, 1), t)
-            for width in (1, 2, 4):
-                t = t + roll(t, width, 1)
+            t = jnp.take_along_axis(t, pick, axis=1, mode="promise_in_bounds")
             m["pe2"][k, pl.ds(0, 8, stride=2), :] = t
             m["pe2"][k, pl.ds(1, 8, stride=2), :] = t
         for i in range(16):

time: 54.8 us -> 53.4 us (0.974)
  Pallas kernels: 52.8 us -> 51.4 us
    pallas_call x1, Pallas kernels: 52.8 us -> 51.4 us  [per_device(): pl.pallas_call(functools.partial(kernel, ngx, ngy, names), out_shape=(sha...]
where the time goes in v4:
time: 53.4 us; the launch traced here: 53.3 us
  Pallas kernels  51.4 us (96%)
  local copies, waits for them, and re-layouts  1.31 us (2%)
  between operations  0.64 us (1%)
    pallas_call x1, Pallas kernels, per_device(): pl.pallas_call(functools.partial(kernel, ngx, ngy, names), out_shape=(sha...  51.4 us
    unnamed x2, local copies, waits for them, and re-layouts  1.31 us

profile of v4, /device:TPU:1, one launch (start us, length us, event | category | flops | bytes accessed | tf_op | source)
XLA Modules:
  0.0 53.3 jit_solution(3399956146096651755)
XLA Ops:
  0.6 51.4 %poisson.1 = (f32[16,16,128]{2,1,0:T(8,128)S(1)}, f32[16,16,128]{2,1,0:T(8,128)S(1)}) custom-call(s32[16,16,128]{2,1,0:T(8,128)} %pc_hbm.1, s32[3,16,16,128]{3,2,1,0:T(8,128)} %fc_hbm.1), custom_call_target="tpu_custom_call" | custom-call | tf_op jit(solution)/shard_map/poisson/pallas_call | solution.py:713
  52.0 0.7 %copy.6 = f32[16,16,128]{2,1,0:T(8,128)} copy(f32[16,16,128]{2,1,0:T(8,128)S(1)} %get-tuple-element.4) | data formatting | bytes 262144
  52.7 0.7 %copy.7 = f32[16,16,128]{2,1,0:T(8,128)} copy(f32[16,16,128]{2,1,0:T(8,128)S(1)} %get-tuple-element.5) | data formatting | bytes 262144

commit v5 on v4

--- a/solution.py
+++ b/solution.py
@@ -401,8 +401,7 @@
     def weight(dg, i, level, off):
         return jnp.where(inside(dg.shape, i, level, off), C1 / dg, 0.0)
 
-    def unpack_in(i):
-        n = 4
+    def unpack_in(n, i):
         for t in range(4):
             part = slice(8 * t, 8 * t + 8)
             pair = m["ext"][pl.ds(i, n), t].astype(F32)
@@ -422,7 +421,7 @@
             m["w0"][pl.ds(i, n), part] = w
             m["x0"][pl.ds(i + 1, n), 8 * t + 8 : 8 * t + 16] = src * w
 
-    sweep(0, 32, 4, unpack_in)
+    sweep(6, 26, 4, functools.partial(unpack_in, 4))
     for t, (py, k) in enumerate(((-1, 1), (0, 0), (0, 1), (1, 0))):
         part = slice(8 * t, 8 * t + 8)
         upper = own_fx[k] if py == 0 else face(0, py, k)[0:8]
@@ -517,8 +516,8 @@
                 out[i, part] = own[r] if (px, py) == (0, 0) else got[from_source(px, py), r]
 
     def pre_level1(c):
-        lv1.first_zero(0, 24, 8)
-        lv1.second_zero(0, 24, 8)
+        lv1.first_zero(2, 22, 10)
+        lv1.second_zero(3, 21, 9)
 
         def store(i, n, r):
             m["r1"][pl.ds(i - 4, n)] = r
@@ -660,15 +659,24 @@
 
     for c in range(2):
         if c == 0:
-            lv0.second_zero(0, 32, 8)
+            lv0.second_zero(7, 25, 6)
         else:
-            lv0.pass_one(4, 28, 8)
-            lv0.pass_two(4, 28, 8)
+            lv0.pass_one(6, 26, 5)
+            lv0.pass_two(7, 25, 6)
         send_b(c)
         if c == 0:
             gather_two(2)
             setup_level1()
             copies_s2 = exchange_tile(EX_S2, m["s2t"], m["rs2"])
+            for lo in (0, 26):
+                sweep(lo, lo + 6, 2, functools.partial(unpack_in, 2))
+            lv0.second_zero(1, 7, 6)
+            lv0.second_zero(25, 31, 6)
+        else:
+            for lo in (4, 26):
+                lv0.pass_one(lo, lo + 2, 2)
+            for lo in (5, 25):
+                lv0.pass_two(lo, lo + 2, 2)
         take_b(c)
         pre_level1(c)
         gather_one(c)
@@ -678,6 +686,11 @@
             assemble(m["s2t"], m["rs2"], m["s2"])
             make_weights(lv2, m["s2"], 8, 16, 6)
         gather_two(c)
+        if c == 0:
+            for at in (1, 22):
+                lv1.first_zero(at, at + 1, 1)
+            for at in (2, 21):
+                lv1.second_zero(at, at + 1, 1)
         arrive(copies_g[c])
         assemble(m["g2t"].at[c], m["rg2"].at[c], m["g2"])
         lv2.first_zero(0, 16, 16)

time: 53.4 us -> 53 us (level)
  no operation moved by 1% of the time
where the time goes in v5:
time: 53 us; the launch traced here: 52.9 us
  Pallas kernels  50.9 us (96%)
  local copies, waits for them, and re-layouts  1.31 us (2%)
  between operations  0.64 us (1%)
    pallas_call x1, Pallas kernels, per_device(): pl.pallas_call(functools.partial(kernel, ngx, ngy, names), out_shape=(sha...  50.9 us
    unnamed x2, local copies, waits for them, and re-layouts  1.31 us

profile of v5, /device:TPU:1, one launch (start us, length us, event | category | flops | bytes accessed | tf_op | source)
XLA Modules:
  0.0 52.9 jit_solution(12380522935317572575)
XLA Ops:
  0.6 50.9 %poisson.1 = (f32[16,16,128]{2,1,0:T(8,128)S(1)}, f32[16,16,128]{2,1,0:T(8,128)S(1)}) custom-call(s32[16,16,128]{2,1,0:T(8,128)} %pc_hbm.1, s32[3,16,16,128]{3,2,1,0:T(8,128)} %fc_hbm.1), custom_call_target="tpu_custom_call" | custom-call | tf_op jit(solution)/shard_map/poisson/pallas_call | solution.py:726
  51.5 0.7 %copy.6 = f32[16,16,128]{2,1,0:T(8,128)} copy(f32[16,16,128]{2,1,0:T(8,128)S(1)} %get-tuple-element.4) | data formatting | bytes 262144
  52.2 0.7 %copy.7 = f32[16,16,128]{2,1,0:T(8,128)} copy(f32[16,16,128]{2,1,0:T(8,128)S(1)} %get-tuple-element.5) | data formatting | bytes 262144
